TPU v7x, 256 devices: a whole 4x4x8 slice. The times are simulated.
256 devices in a mesh: sib: 8 (over z), ctx: 8 (over x, core), head: 4 (over y).
Axes of the slice: x: 4, y: 4, z: 8, core: 2. Of those that a mesh axis runs over, the one named last changes fastest.
Arguments:
- queries: bfloat16 [8, 4096, 4, 1536], P('sib', 'ctx', 'head'), may hold values from -8 to 8
- suffix_kv: bfloat16 [8, 4096, 4, 320], P('sib', 'ctx', 'head'), may hold values from -6 to 6
- prefix_kv: bfloat16 [131072, 4, 320], P(('sib', 'ctx'), 'head'), may hold values from -6 to 6
- pooling: float32 [2, 64], replicated, may hold values from 0.03 to 0.3
- gate_logits: float32 [8, 4096, 4, 24], P('sib', 'ctx', 'head'), may hold values from -6 to 6
- selected: int32 [8, 64, 4, 16], P('sib', 'ctx', 'head'), may hold values from 0 to 2047, as said below
- lengths: int32 [8], P('sib'), may hold values from 512 to 4096, as said below
- w_out: bfloat16 [4096, 2560], P('head'), may hold values from -0.375 to 0.375
Outputs:
- layer_out: bfloat16 [8, 4096, 2560], P('sib', ('ctx', 'head'))
Inputs may be any that keep to these rules, and one draw needn't show every extreme that they name: For each sibling and group, the 16 indices of a query block are distinct, and the query blocks of one index of ctx (8 aligned query blocks) select together at most 3 blocks, counted with repeats, among any aligned range of 32 prefix blocks; some range is selected exactly 3 times in every such run. `lengths`: some sibling has the full length 4096 and some the length 512.
All inputs are finite; a program needn't handle non-finite values.
Results may differ from a plain program's by a relative error of at most 0.0096.
Values may be sent and summed in bfloat16 or wider, within the bound.
A program may use at most 192 MiB of HBM per device.

v0:
```python
import jax
import jax.numpy as jnp
from jax import lax
from jax.sharding import PartitionSpec as P

DK = 192
DV = 128
HQ = 8
DM = 2560
BLK = 64
W = 512


def passed_along(value, axis, steps):
    count = lax.axis_size(axis)
    first, last = (max(0, -steps), min(count, count - steps))
    return lax.ppermute(value, axis, [(source, source + steps) for source in range(first, last)])


def earlier_rows(own_kv, distance):
    return passed_along(own_kv, "ctx", distance)


def softmax_parts(scores):
    row_max = jnp.max(scores, axis=-1, keepdims=True)
    weights = jnp.exp(scores - row_max)
    return (weights.astype(jnp.bfloat16), jnp.sum(weights, axis=-1, keepdims=True))


def shards(queries, suffix_kv, prefix_kv, pooling, gate_logits, selected, lengths, w_out):
    row_count = queries.shape[1]
    score_scale = DK ** (-0.5)
    query_rows = queries.reshape(row_count, HQ, DK)
    owned_blocks = prefix_kv.reshape(-1, BLK, DK + DV)
    block_count = owned_blocks.shape[0]
    owned_float = owned_blocks.astype(jnp.float32)
    comp_keys = jnp.einsum(
        "bjd,j->bd", owned_float[:, :, :DK], pooling[0], precision=lax.Precision.HIGHEST
    )
    comp_values = jnp.einsum(
        "bjd,j->bd", owned_float[:, :, DK:], pooling[1], precision=lax.Precision.HIGHEST
    )
    compressed = jnp.concatenate([comp_keys, comp_values], axis=-1).astype(jnp.bfloat16)
    segment = lax.all_gather(compressed, ("sib", "ctx"), axis=0, tiled=True)
    row_max = jnp.full((row_count, HQ), -1e30, jnp.float32)
    scores = (
        jnp.einsum("rhd,kd->rhk", query_rows, segment[:, :DK], preferred_element_type=jnp.float32)
        * score_scale
    )
    new_max = jnp.maximum(row_max, jnp.max(scores, axis=-1))
    weights = jnp.exp(scores - new_max[:, :, None])
    row_total = jnp.sum(weights, axis=-1)
    accumulated = jnp.einsum(
        "rhk,kd->rhd",
        weights.astype(jnp.bfloat16),
        segment[:, DK:],
        preferred_element_type=jnp.float32,
    )
    row_max, row_total, accumulated = (new_max, row_total, accumulated)
    comp_out = accumulated / row_total[:, :, None]
    own_kv = suffix_kv.reshape(row_count, DK + DV)
    window_reach = -(-W // row_count)
    near_parts = [earlier_rows(own_kv, 1)]
    near_kv = jnp.concatenate(near_parts + [own_kv], axis=0)
    row_begin = lax.axis_index("ctx") * row_count
    query_pos = row_begin + jnp.arange(row_count, dtype=jnp.int32)
    key_pos = (
        row_begin
        - window_reach * row_count
        + jnp.arange((window_reach + 1) * row_count, dtype=jnp.int32)
    )
    visible = (
        (key_pos[None, :] <= query_pos[:, None])
        & (key_pos[None, :] > query_pos[:, None] - W)
        & (key_pos[None, :] >= 0)
    )
    scores = (
        jnp.einsum("rhd,kd->rhk", query_rows, near_kv[:, :DK], preferred_element_type=jnp.float32)
        * score_scale
    )
    scores = jnp.where(visible[:, None, :], scores, -jnp.inf)
    weights, window_total = softmax_parts(scores)
    win_out = (
        jnp.einsum("rhk,kd->rhd", weights, near_kv[:, DK:], preferred_element_type=jnp.float32)
        / window_total
    )
    slot_ids = selected.reshape(-1)
    slot_count = slot_ids.shape[0]
    owner_count = lax.axis_size("sib") * lax.axis_size("ctx")
    capacity = max(2, (slot_count * 3 // 2 + owner_count - 1) // owner_count)
    slot_owner = slot_ids // block_count
    slot_local = slot_ids % block_count
    owner_match = (slot_owner[:, None] == jnp.arange(owner_count, dtype=jnp.int32)[None, :]).astype(
        jnp.int32
    )
    slot_rank = jnp.sum((jnp.cumsum(owner_match, axis=0) - 1) * owner_match, axis=1)
    slot_place = slot_owner * capacity + slot_rank
    place_match = (
        slot_place[:, None] == jnp.arange(owner_count * capacity, dtype=jnp.int32)[None, :]
    ).astype(jnp.int32)
    requests = (jnp.sum(place_match * (slot_local[:, None] + 1), axis=0) - 1).reshape(
        owner_count, capacity
    )
    wanted = lax.all_to_all(requests, ("sib", "ctx"), split_axis=0, concat_axis=0, tiled=True)
    served = jnp.take(owned_blocks, jnp.maximum(wanted, 0), axis=0)
    received = lax.all_to_all(served, ("sib", "ctx"), split_axis=0, concat_axis=0, tiled=True)
    picked = jnp.take(received.reshape(owner_count * capacity, BLK, DK + DV), slot_place, axis=0)
    blocks_here = row_count // BLK
    picked = picked.reshape(blocks_here, -1, DK + DV)
    query_blocks = query_rows.reshape(blocks_here, BLK, HQ, DK)
    scores = (
        jnp.einsum(
            "qthd,qkd->qhtk", query_blocks, picked[:, :, :DK], preferred_element_type=jnp.float32
        )
        * score_scale
    )
    weights, selected_total = softmax_parts(scores)
    sel_out = (
        jnp.einsum("qhtk,qkd->qhtd", weights, picked[:, :, DK:], preferred_element_type=jnp.float32)
        / selected_total
    )
    sel_out = jnp.transpose(sel_out, (0, 2, 1, 3)).reshape(row_count, HQ, DV)
    gate_values = jax.nn.sigmoid(gate_logits.reshape(row_count, 3, HQ))
    head_out = (
        gate_values[:, 0, :, None] * comp_out
        + gate_values[:, 1, :, None] * sel_out
        + gate_values[:, 2, :, None] * win_out
    )
    head_out = jnp.where((query_pos < lengths[0])[:, None, None], head_out, 0.0)
    head_flat = head_out.astype(jnp.bfloat16).reshape(row_count, HQ * DV)
    summed = lax.psum_scatter(
        jnp.dot(head_flat, w_out, preferred_element_type=jnp.float32),
        "head",
        scatter_dimension=0,
        tiled=True,
    )
    return summed.astype(jnp.bfloat16).reshape(1, -1, DM)


def solution(mesh):
    return jax.shard_map(
        shards,
        mesh=mesh,
        in_specs=(
            P("sib", "ctx", "head", None),
            P("sib", "ctx", "head", None),
            P(("sib", "ctx"), "head", None),
            P(),
            P("sib", "ctx", "head", None),
            P("sib", "ctx", "head", None),
            P("sib"),
            P("head", None),
        ),
        out_specs=P("sib", ("ctx", "head"), None),
        check_vma=False,
    )
```

profile of v0, /device:TPU:1, one launch (start us, length us, event | category | flops | bytes accessed | tf_op | source)
XLA Modules:
  0.0 388.3 jit_solution(3440374522089827407)
XLA Ops:
  7.0 1.3 reduce.9
  9.1 0.8 sub.57
  9.8 13.0 %all-to-all-start = ((s32[64,1,3]{2,1,0:T(1,128)}), s32[64,1,3]{2,1,0:T(1,128)S(1)}, u32[]{:S(2)}, u32[]{:S(2)}) async-start(s32[64,1,3]{2,1,0:T(1,128)} %bitcast.17), calls=%async_computation | async-start | bytes 65536 | tf_op jit(solution)/shard_map/all_to_all | solution.py:104
  22.8 1.8 copy.51
  24.6 7.5 %all-to-all-done = s32[64,1,3]{2,1,0:T(1,128)S(1)} async-done(((s32[64,1,3]{2,1,0:T(1,128)}), s32[64,1,3]{2,1,0:T(1,128)S(1)}, u32[]{:S(2)}, u32[]{:S(2)}) %all-to-all-start) | async-done | bytes 800 | tf_op jit(solution)/shard_map/all_to_all | solution.py:104
  32.7 10.0 %gather_fusion = bf16[192,64,320]{2,1,0:T(8,128)(2,1)} fusion(bf16[32,64,320]{2,1,0:T(8,128)(2,1)S(1)} %bitcast.121, s32[1024]{0:T(1024)S(1)} %pad_clamp_fusion.1), kind=kCustom, calls=%fused_computation | custom fusion | bytes 15729408 | tf_op jit(solution)/shard_map/jit(_take)/gather | solution.py:105
  42.7 8.4 %broadcast_select_fusion = bf16[64,3,64,320]{3,2,1,0:T(8,128)(2,1)} fusion(bf16[64,3,64,320]{3,2,1,0:T(8,128)(2,1)} %bitcast.124, pred[64,3]{1,0:T(8,128)(4,1)S(1)} %copy.58), kind=kLoop, calls=%fused_computation.18 | loop fusion | flops 3932160 | bytes 15728832 | tf_op jit(solution)/shard_map/jit(_take)/select_n | solution.py:105
  51.1 5.9 %all-to-all-start.1 = ((bf16[64,3,64,320]{3,2,1,0:T(8,128)(2,1)}), bf16[64,3,64,320]{3,2,1,0:T(8,128)(2,1)}, u32[]{:S(2)}, u32[]{:S(2)}) async-start(bf16[64,3,64,320]{3,2,1,0:T(8,128)(2,1)} %broadcast_select_fusion), calls=%async_computation.1 | async-start | bytes 18874368 | tf_op jit(solution)/shard_map/all_to_all | solution.py:106
  58.9 3.7 collective-permute-start
  62.7 3.3 reshape_reshape.3
  66.0 2.6 copy.53
  70.2 0.8 and_and_fusion
  71.1 14.4 %collective-permute-done = bf16[512,320]{0,1:T(8,128)(2,1)S(1)} collective-permute-done((bf16[512,320]{0,1:T(8,128)(2,1)S(1)}, bf16[512,320]{0,1:T(8,128)(2,1)S(1)}, u32[]{:S(2)}, u32[]{:S(2)}) %collective-permute-start) | collective-permute-done | bytes 327712 | tf_op jit(solution)/shard_map/ppermute | solution.py:17
  85.5 9.3 %fusion.10 = (f32[512,8]{0,1:T(8,128)S(1)}, f32[1024,512,8]{1,0,2:T(8,128)}) fusion(pred[512,1024]{0,1:T(8,128)(4,1)S(1)} %and_and_fusion, bf16[512,8,192]{0,2,1:T(8,128)(2,1)} %bitcast.129, bf16[512,320]{0,1:T(8,128)(2,1)S(1)} %bitcast.140, bf16[512,320]{0,1:T(8,128)(2,1)S(1)} %collective-permute-done), kind=kOutput, calls=%fused_computation.17 | convolution fusion | flops 1623977984 | bytes 19546112 | tf_op jit(solution)/shard_map/rhd,kd->rhk/dot_general | solution.py:78
  94.8 9.2 %fusion.6 = f32[512,8]{0,1:T(8,128)S(1)} fusion(f32[1024,512,8]{1,0,2:T(8,128)} %get-tuple-element.15, f32[512,8]{0,1:T(8,128)S(1)} %get-tuple-element.14, pred[512,1024]{0,1:T(8,128)(4,1)S(1)} %and_and_fusion), kind=kLoop, calls=%fused_computation.13 | loop fusion | flops 16773120 | bytes 17334272 | tf_op jit(solution)/shard_map/reduce_sum | solution.py:27
  103.9 55.9 %all-gather.2.cloned.1.call-done = bf16[2048,320]{1,0:T(8,128)(2,1)} async-done(((bf16[32,320]{1,0:T(8,128)(2,1)}), bf16[2048,320]{1,0:T(8,128)(2,1)}) %all-gather.2.cloned.1.call-update) | async-done | bytes 1310736 | tf_op jit(solution)/shard_map/all_gather | solution.py:44
  159.8 17.3 %bitcast_reduce_fusion = (f32[512,8]{0,1:T(8,128)S(1)}, f32[2048,512,8]{1,0,2:T(8,128)}) fusion(bf16[512,8,192]{0,2,1:T(8,128)(2,1)} %bitcast.130, bf16[2048,320]{1,0:T(8,128)(2,1)} %all-gather.2.cloned.1.call-done), kind=kOutput, calls=%fused_computation.3 | convolution fusion | flops 3237998592 | bytes 36192256 | tf_op jit(solution)/shard_map/rhd,kd->rhk/dot_general | solution.py:47
  177.1 15.6 %fusion.4 = f32[512,8,128]{0,2,1:T(8,128)} fusion(f32[2048,512,8]{1,0,2:T(8,128)} %get-tuple-element.13, f32[512,8]{0,1:T(8,128)S(1)} %broadcast_maximum_fusion, bf16[2048,320]{1,0:T(8,128)(2,1)} %all-gather.2.cloned.1.call-done), kind=kOutput, calls=%fused_computation.12 | convolution fusion | flops 2172649472 | bytes 36192256 | tf_op jit(solution)/shard_map/rhk,kd->rhd/dot_general | solution.py:53
  192.8 13.8 %fusion.1 = f32[512,8]{0,1:T(8,128)S(1)} fusion(f32[2048,512,8]{1,0,2:T(8,128)} %get-tuple-element.13, f32[512,8]{0,1:T(8,128)S(1)} %broadcast_maximum_fusion), kind=kLoop, calls=%fused_computation.5 | loop fusion | flops 25161728 | bytes 33587200 | tf_op jit(solution)/shard_map/reduce_sum | solution.py:52
  206.6 60.3 %all-to-all-done.1 = bf16[64,3,64,320]{3,2,1,0:T(8,128)(2,1)} async-done(((bf16[64,3,64,320]{3,2,1,0:T(8,128)(2,1)}), bf16[64,3,64,320]{3,2,1,0:T(8,128)(2,1)}, u32[]{:S(2)}, u32[]{:S(2)}) %all-to-all-start.1) | async-done | bytes 7864352 | tf_op jit(solution)/shard_map/all_to_all | solution.py:106
  266.8 7.7 %gather_fusion.1 = bf16[128,64,320]{2,1,0:T(8,128)(2,1)} fusion(bf16[192,64,320]{2,1,0:T(8,128)(2,1)} %bitcast.20, s32[1024]{0:T(1024)S(1)} %pad_clamp_fusion), kind=kCustom, calls=%fused_computation.1 | custom fusion | bytes 10486272 | tf_op jit(solution)/shard_map/jit(_take)/gather | solution.py:107
  274.6 8.2 %copy.59 = bf16[8,1024,320]{1,2,0:T(8,128)(2,1)} copy(bf16[8,1024,320]{2,1,0:T(8,128)(2,1)} %bitcast.125) | data formatting | bytes 10485760 | tf_op jit(solution)/shard_map/jit(_take)/gather | solution.py:107
  282.8 5.4 %broadcast_select_fusion.1 = bf16[8,1024,320]{1,2,0:T(8,128)(2,1)} fusion(bf16[8,1024,320]{1,2,0:T(8,128)(2,1)} %copy.59, pred[8,1024]{1,0:T(8,128)(4,1)S(1)} %broadcast_in_dim.72), kind=kLoop, calls=%fused_computation.24 | loop fusion | flops 2621440 | bytes 10493952 | tf_op jit(solution)/shard_map/jit(_take)/select_n | solution.py:107
  288.2 4.1 %bitcast_reduce_fusion.1 = (f32[8,8,64]{2,1,0:T(8,128)S(1)}, f32[8,1024,64,8]{1,2,3,0:T(8,128)S(1)}) fusion(bf16[8,64,8,192]{3,2,1,0:T(8,128)(2,1)S(1)} %reshape_reshape.3, bf16[8,1024,320]{1,2,0:T(8,128)(2,1)} %broadcast_select_fusion.1), kind=kOutput, calls=%fused_computation.9 | convolution fusion | flops 1618997248 | bytes 21512192 | tf_op jit(solution)/shard_map/qthd,qkd->qhtk/dot_general | solution.py:112
  292.3 3.7 fusion.8
  296.0 4.5 %bitcast_divide_fusion = f32[8,64,8,128]{3,1,2,0:T(8,128)} fusion(bf16[8,1024,320]{1,2,0:T(8,128)(2,1)S(1)} %copy-done, f32[8,1024,64,8]{1,2,3,0:T(8,128)S(1)} %get-tuple-element.11, f32[8,8,64]{2,1,0:T(8,128)S(1)} %get-tuple-element.10, f32[8,64,8]{1,2,0:T(8,128)S(1)} %bitcast.136), kind=kOutput, calls=%fused_computation.28 | convolution fusion | flops 1086849024 | bytes 21037056 | tf_op jit(solution)/shard_map/qhtk,qkd->qhtd/dot_general | solution.py:119
  300.5 2.8 copy.62
  303.3 1.9 copy.63
  305.2 9.7 %select_convert_fusion = bf16[512,8,128]{0,2,1:T(8,128)(2,1)S(1)} fusion(f32[512,8,128]{0,2,1:T(8,128)} %copy.63, f32[512,8,128]{0,2,1:T(8,128)} %fusion.4, f32[512,8]{0,1:T(8,128)S(1)} %fusion.6, f32[512,8]{0,1:T(8,128)S(1)} %get-tuple-element.6, f32[512,8]{0,1:T(8,128)S(1)} %get-tuple-element.7, f32[512,8]{0,1:T(8,128)S(1)} %fusion.1, ...), kind=kOutput, calls=%fused_computation.30 | convolution fusion | flops 1095761920 | bytes 23298560 | tf_op jit(solution)/shard_map/rhk,kd->rhd/dot_general | solution.py:84
  315.0 4.7 %fusion.54 = f32[512,2560]{1,0:T(8,128)} fusion(bf16[512,1024]{0,1:T(8,128)(2,1)S(1)} %bitcast.131, bf16[1024,2560]{1,0:T(8,128)(2,1)S(1)} %bitcast.128), kind=kOutput, calls=%fused_computation.104 | convolution fusion | flops 2684354560 | bytes 11534336 | tf_op jit(solution)/shard_map/dot_general | solution.py:132
  319.7 59.6 %reduce-scatter.2.cloned.1.call-done = f32[128,2560]{1,0:T(8,128)} async-done(((f32[512,2560]{1,0:T(8,128)}), f32[128,2560]{1,0:T(8,128)}) %reduce-scatter.2.cloned.1.call-update) | async-done | bytes 1310736 | tf_op jit(solution)/shard_map/reduce_scatter | solution.py:131
  379.2 2.2 convert_bitcast_fusion
  (59 shorter events, 4.5 us)
Async XLA Ops:
  9.8 22.3 %all-to-all-start = ((s32[64,1,3]{2,1,0:T(1,128)}), s32[64,1,3]{2,1,0:T(1,128)S(1)}, u32[]{:S(2)}, u32[]{:S(2)}) async-start(s32[64,1,3]{2,1,0:T(1,128)} %bitcast.17), calls=%async_computation | async-start | bytes 65536 | tf_op jit(solution)/shard_map/all_to_all | solution.py:104
  51.1 6.0 %copy-start.4 = (f32[2,64]{1,0:T(2,128)S(1)}, f32[2,64]{1,0:T(2,128)}, u32[]{:S(2)}) copy-start(f32[2,64]{1,0:T(2,128)} %param.11) | copy-start | bytes 1540
  51.1 7.8 %copy-start.5 = (bf16[1,512,1,320]{1,3,2,0:T(8,128)(2,1)S(1)}, bf16[1,512,1,320]{1,3,2,0:T(8,128)(2,1)}, u32[]{:S(2)}) copy-start(bf16[1,512,1,320]{1,3,2,0:T(8,128)(2,1)} %param.9) | copy-start | bytes 983044
  51.1 215.8 %all-to-all-start.1 = ((bf16[64,3,64,320]{3,2,1,0:T(8,128)(2,1)}), bf16[64,3,64,320]{3,2,1,0:T(8,128)(2,1)}, u32[]{:S(2)}, u32[]{:S(2)}) async-start(bf16[64,3,64,320]{3,2,1,0:T(8,128)(2,1)} %broadcast_select_fusion), calls=%async_computation.1 | async-start | bytes 18874368 | tf_op jit(solution)/shard_map/all_to_all | solution.py:106
  57.0 11.6 %copy-start.3 = (s32[1,8,1,16]{3,2,1,0:T(1,128)S(1)}, s32[1,8,1,16]{3,2,1,0:T(1,128)}, u32[]{:S(2)}) copy-start(s32[1,8,1,16]{3,2,1,0:T(1,128)} %param.13) | copy-start | bytes 1540
  57.0 12.6 %copy-start.2 = (f32[1,512,1,24]{1,3,2,0:T(8,128)S(1)}, f32[1,512,1,24]{1,3,2,0:T(8,128)}, u32[]{:S(2)}) copy-start(f32[1,512,1,24]{1,3,2,0:T(8,128)} %param.12) | copy-start | bytes 147460
  57.0 102.8 %all-gather.2.cloned.1.call-start = ((), (), s32[]{:S(2)}) async-start(), calls=%async_computation.3 | async-start | bytes 1597440 | tf_op jit(solution)/shard_map/all_gather | solution.py:44
  58.8 320.4 %reduce-scatter.2.cloned.1.call-start = ((), (), s32[]{:S(2)}) async-start(), calls=%async_computation.4 | async-start | bytes 6553600 | tf_op jit(solution)/shard_map/reduce_scatter | solution.py:131
  58.9 26.6 %collective-permute-start = (bf16[512,320]{0,1:T(8,128)(2,1)S(1)}, bf16[512,320]{0,1:T(8,128)(2,1)S(1)}, u32[]{:S(2)}, u32[]{:S(2)}) collective-permute-start(bf16[512,320]{0,1:T(8,128)(2,1)S(1)} %bitcast.139), channel_id=1, source_target_pairs={{0,4},{4,8},{8,12},{12,16},{16,20},{20,24},{24,28},{1,5},{5,9},{9,... | collective-permute-start | bytes 983048 | tf_op jit(solution)/shard_map/ppermute | solution.py:17
  71.1 23.7 %copy-start.1 = (pred[512,1024]{0,1:T(8,128)(4,1)}, pred[512,1024]{0,1:T(8,128)(4,1)S(1)}, u32[]{:S(2)}) copy-start(pred[512,1024]{0,1:T(8,128)(4,1)S(1)} %and_and_fusion) | copy-start | bytes 1572868
  85.5 9.3 %copy-start.6 = (bf16[512,320]{0,1:T(8,128)(2,1)}, bf16[512,320]{0,1:T(8,128)(2,1)S(1)}, u32[]{:S(2)}) copy-start(bf16[512,320]{0,1:T(8,128)(2,1)S(1)} %collective-permute-done) | copy-start | bytes 983044
  292.3 3.7 copy-start
  300.5 4.7 %copy-start.7 = (pred[512]{0:T(512)(128)(4,1)S(1)}, pred[512]{0:T(512)(128)(4,1)}, u32[]{:S(2)}) copy-start(pred[512]{0:T(512)(128)(4,1)} %fusion.41) | copy-start | bytes 1540
  303.3 11.6 %slice-start = ((s8[5242880]{0:T(1024)(128)(4,1)}), s8[1048576]{0:T(1024)(128)(4,1)S(1)}, s32[]{:S(2)}) async-start(s8[5242880]{0:T(1024)(128)(4,1)} %bitcast.127), calls=%async_computation.5 | async-start | bytes 2097152
  305.2 9.7 %slice-start.1 = ((s8[5242880]{0:T(1024)(128)(4,1)}), s8[4194304]{0:T(1024)(128)(4,1)S(1)}, s32[]{:S(2)}) async-start(s8[5242880]{0:T(1024)(128)(4,1)} %bitcast.127), calls=%async_computation.6 | async-start | bytes 8388608
Sparse Core Ops, SparseCore 0:
  60.6 99.1 all-gather.1
  319.8 59.3 reduce-scatter.1
where the time goes:
time: 389 us; the launch traced here: 388 us
  waiting for transfers between devices  198 us (51%)
  matrix products  66.2 us (17%)
  other arithmetic  46.9 us (12%)
  local copies, waits for them, and re-layouts  40.4 us (10%)
  starting transfers between devices  22.7 us (6%)
  between operations  14.4 us (4%)
    all_to_all x1, waiting for transfers between devices, shards(): lax.all_to_all(served, ('sib', 'ctx'), split_axis=0, concat_axis=0, tiled...  60.3 us
    reduce_scatter x1, waiting for transfers between devices, shards(): lax.psum_scatter(jnp.dot(head_flat, w_out, preferred_element_type=jnp.flo...  59.6 us
    all_gather x1, waiting for transfers between devices, shards(): segment = lax.all_gather(compressed, ('sib', 'ctx'), axis=0, tiled=True)  55.9 us
    dot_general x1, matrix products, shards(): jnp.einsum('rhd,kd->rhk', query_rows, segment[:, :DK], preferred_element_...  17.3 us
    gather x2, local copies, waits for them, and re-layouts, shards(): jnp.take(received.reshape(owner_count * capacity, BLK, DK + DV), slot_pla...  16 us
    dot_general x1, matrix products, shards(): jnp.einsum('rhk,kd->rhd', weights.astype(jnp.bfloat16), segment[:, DK:],...  15.6 us
    ppermute x1, waiting for transfers between devices, passed_along(): lax.ppermute(value, axis, [(source, source + steps) for source in range(f...  14.4 us
    reduce_sum x1, other arithmetic, shards(): row_total = jnp.sum(weights, axis=-1)  13.8 us
  transfers between devices with their start and end apart: 5, of which 5 were waited for; matrix products, arithmetic and copies ran while one was open for 20% of the time, Pallas kernels for 0%

commit v1 on v0

v1 whole, which is shorter than its diff:
```python
import functools

import jax
import jax.numpy as jnp
from jax import lax
from jax.experimental import pallas as pl
from jax.experimental.pallas import tpu as pltpu
from jax.sharding import PartitionSpec as P

DK = 192
DV = 128
KV = DK + DV
HQ = 8
DM = 2560
BLK = 64
W = 512
ROWS = 512
NB = 32
TOPK = 16
QB = ROWS // BLK
NZ = 8
NC = 8
CAP = 3
PAIRS = NB // 2
CHUNK = 4
LANES = 128
TILE = HQ * BLK
SCALE2 = DK ** (-0.5) * 1.4426950408889634
MESH = pl.DeviceIdType.MESH
BF16 = jnp.bfloat16
F32 = jnp.float32


def remote(source, target, send_sem, recv_sem, device):
    return pltpu.make_async_remote_copy(
        src_ref=source,
        dst_ref=target,
        send_sem=send_sem,
        recv_sem=recv_sem,
        device_id=device,
        device_id_type=MESH,
    )


def swap_halves(tile):
    return jnp.concatenate([tile[:, 64:], tile[:, :64]], axis=1)


def layer_kernel(
    pos_ref,
    len_ref,
    q_ref,
    suffix_ref,
    prefix_ref,
    comp_ref,
    request_ref,
    gate_ref,
    out_ref,
    own,
    plus1,
    plus2,
    plus3,
    minus1,
    minus2,
    minus3,
    far,
    outgoing,
    incoming,
    comp_all,
    near,
    asked,
    asked_smem,
    q_raw,
    q_heads,
    mixed,
    sel_kv,
    load_sem,
    misc_sem,
    z_send,
    z_recv,
    x_send,
    x_recv,
    comp_send,
    comp_recv,
    ask_send,
    ask_recv,
    ask_load,
    halo_send,
    halo_recv,
):
    z = lax.axis_index("sib")
    c = lax.axis_index("ctx")
    y = lax.axis_index("head")

    def z_peer(offset):
        return ((z + offset) % NZ, c, y)

    def c_peer(offset):
        return (z, (c + offset) % NC, y)

    barrier = pltpu.get_barrier_semaphore()
    for offset in range(1, NZ):
        pl.semaphore_signal(barrier, inc=1, device_id=z_peer(offset), device_id_type=MESH)
    for offset in range(1, NC):
        pl.semaphore_signal(barrier, inc=1, device_id=c_peer(offset), device_id_type=MESH)

    loads = [
        pltpu.make_async_copy(
            prefix_ref.at[:, pl.ds(pair * LANES, LANES)], own.at[pair], load_sem.at[pair]
        )
        for pair in range(PAIRS)
    ]
    for load in loads:
        load.start()
    q_load = pltpu.make_async_copy(q_ref, q_raw, misc_sem.at[0])
    q_load.start()
    near_load = pltpu.make_async_copy(suffix_ref, near.at[:, pl.ds(ROWS, ROWS)], misc_sem.at[1])
    near_load.start()
    comp_load = pltpu.make_async_copy(comp_ref, comp_all.at[0, 0], misc_sem.at[2])
    comp_load.start()
    ask_self = pltpu.make_async_copy(request_ref.at[0], asked_smem.at[0], ask_load.at[0])
    ask_self.start()
    pl.semaphore_wait(barrier, NZ - 1 + NC - 1)

    def comp_over_z(offset):
        return remote(
            comp_ref,
            comp_all.at[0, NZ - offset],
            comp_send.at[0, offset],
            comp_recv.at[0, NZ - offset],
            z_peer(offset),
        )

    def comp_over_c(offset):
        return remote(
            comp_all.at[0],
            comp_all.at[NC - offset],
            comp_send.at[1, offset],
            comp_recv.at[1, NC - offset],
            c_peer(offset),
        )

    def ask(offset):
        return remote(
            request_ref.at[offset],
            asked.at[NC - offset],
            ask_send.at[offset],
            ask_recv.at[NC - offset],
            c_peer(offset),
        )

    def halo():
        return remote(
            suffix_ref, near.at[:, pl.ds(0, ROWS)], halo_send.at[0], halo_recv.at[0], c_peer(1)
        )

    stages = {1: (own, plus1, plus2, plus3, far), -1: (own, minus1, minus2, minus3, far)}

    def z_chunks(way, step):
        if step < 3:
            return tuple(range(4))
        return (0, 1) if way == 1 else (2, 3)

    def z_copy(way, step, chunk):
        row = 0 if way == 1 else 1
        window = pl.ds(CHUNK * chunk, CHUNK)
        return remote(
            stages[way][step].at[window],
            stages[way][step + 1].at[window],
            z_send.at[row, step, chunk],
            z_recv.at[row, step, chunk],
            z_peer(way),
        )

    def x_copy(plane, offset):
        return remote(
            outgoing.at[pl.ds((plane * NC + offset) * CAP, CAP)],
            incoming.at[pl.ds((plane * NC + NC - offset) * CAP, CAP)],
            x_send.at[plane, offset],
            x_recv.at[plane, NC - offset],
            c_peer(offset),
        )

    left_half = lax.broadcasted_iota(jnp.int32, (KV // 2, LANES), 1) < BLK

    planes = {0: own, 7: plus1, 6: plus2, 5: plus3, 1: minus1, 2: minus2, 3: minus3, 4: far}

    def fill(plane):
        held = planes[plane]

        def one(index, carry):
            offset = index // CAP
            slot = index % CAP
            pair = asked_smem[offset, plane, slot]
            half = asked_smem[offset, plane, CAP + slot]
            tile = held[pair]
            upper = tile[: KV // 2]
            lower = tile[KV // 2 :]
            first = half == 0
            kept_upper = jnp.where(first, upper, swap_halves(upper))
            kept_lower = jnp.where(first, swap_halves(lower), lower)
            outgoing[plane * NC * CAP + index] = jnp.where(left_half, kept_upper, kept_lower)
            return carry

        lax.fori_loop(0, NC * CAP, one, 0)
        base = plane * NC * CAP
        incoming[pl.ds(base, CAP)] = outgoing[pl.ds(base, CAP)]

    def send_plane(plane):
        for offset in (2, 6, 4, 3, 5, 1, 7):
            x_copy(plane, offset).start()

    def forward(step, chunk):
        for way in (1, -1):
            if chunk in z_chunks(way, step):
                z_copy(way, step, chunk).wait_recv()
                if step < 3 and chunk in z_chunks(way, step + 1):
                    z_copy(way, step + 1, chunk).start()

    for offset in (4, 3, 5, 2, 6, 1, 7):
        comp_over_z(offset).start()
    for offset in range(1, NC):
        ask(offset).start()
    halo().start()
    for load in loads:
        load.wait()
    for chunk in range(4):
        for way in (1, -1):
            z_copy(way, 0, chunk).start()

    q_load.wait()
    for head in range(HQ):
        q_heads[head] = q_raw[:, head * DK : (head + 1) * DK]

    for offset in range(1, NC):
        ask(NC - offset).wait_recv()
        pltpu.make_async_copy(asked.at[offset], asked_smem.at[offset], ask_load.at[offset]).start()
    comp_load.wait()
    for offset in range(1, NZ):
        comp_over_z(NZ - offset).wait_recv()
    for offset in (4, 2, 6, 3, 5, 1, 7):
        comp_over_c(offset).start()
    for offset in range(1, NC):
        pltpu.make_async_copy(asked.at[offset], asked_smem.at[offset], ask_load.at[offset]).wait()
    ask_self.wait()
    fill(0)

    def queries_of(block):
        rows = pl.ds(pl.multiple_of(block * BLK, BLK), BLK)
        return q_heads[:, rows, :].reshape(TILE, DK)

    def gate_columns(block):
        rows = pl.ds(pl.multiple_of(block * BLK, BLK), BLK)
        return gate_ref[rows, :]

    def softmax(scores, previous_max=None):
        top = jnp.max(scores, axis=-1, keepdims=True)
        if previous_max is not None:
            top = jnp.maximum(previous_max, top)
        weights = jnp.exp2(scores * SCALE2 - top * SCALE2)
        return top, weights, jnp.sum(weights, axis=-1, keepdims=True)

    nt = (((1,), (1,)), ((), ()))

    near_load.wait()
    halo().wait_recv()

    def window_block(block, carry):
        start = pl.multiple_of((block // 2) * LANES, LANES)
        span = pl.ds(start, W + LANES)
        scores = jnp.dot(queries_of(block), near[:DK, span], preferred_element_type=F32)
        scores = scores.reshape(HQ, BLK, W + LANES)
        row = lax.broadcasted_iota(jnp.int32, (1, BLK, W + LANES), 1) + (block % 2) * BLK
        lane = lax.broadcasted_iota(jnp.int32, (1, BLK, W + LANES), 2)
        reach = jnp.where(c == 0, ROWS - start, 0)
        visible = (lane > row) & (lane <= row + W) & (lane >= reach)
        scores = jnp.where(visible, scores, -jnp.inf).reshape(TILE, W + LANES)
        _, weights, total = softmax(scores)
        result = lax.dot_general(
            weights.astype(BF16), near[DK:, span], nt, preferred_element_type=F32
        )
        result = result / total
        gates = gate_columns(block)
        for head in range(HQ):
            mixed[block, head * BLK : (head + 1) * BLK, :] = (
                result[head * BLK : (head + 1) * BLK]
                * gates[:, 2 * HQ + head : 2 * HQ + head + 1]
            )
        return carry

    window_block(0, 0)
    send_plane(0)

    def window_loop(block, carry):
        window_block(block, carry)

        @pl.when(block == 2)
        def _():
            forward(0, 0)

        @pl.when(block == 4)
        def _():
            forward(0, 1)

        @pl.when(block == 6)
        def _():
            forward(0, 2)

        return carry

    lax.fori_loop(1, QB, window_loop, 0)

    for offset in range(1, NC):
        comp_over_c(NC - offset).wait_recv()

    half_keys = NZ * NC * NB // 2

    def comp_block(block, carry):
        queries = queries_of(block)
        comp_flat = comp_all.reshape(NZ * NC * NB, 3 * LANES)
        top = None
        for part in range(2):
            keys = pl.ds(part * half_keys, half_keys)
            scores = lax.dot_general(
                queries, comp_flat[keys, :DK], nt, preferred_element_type=F32
            )
            new_top, weights, total = softmax(scores, top)
            result = jnp.dot(
                weights.astype(BF16), comp_flat[keys, 2 * LANES :], preferred_element_type=F32
            )
            if part == 0:
                top, all_total, all_result = new_top, total, result
            else:
                decay = jnp.exp2((top - new_top) * SCALE2)
                all_total = all_total * decay + total
                all_result = all_result * decay + result
        result = all_result / all_total
        gates = gate_columns(block)
        for head in range(HQ):
            rows = slice(head * BLK, (head + 1) * BLK)
            mixed[block, rows, :] += result[rows] * gates[:, head : head + 1]
        return carry

    def comp_loop(block, carry):
        comp_block(block, carry)

        @pl.when(block == 0)
        def _():
            forward(0, 3)
            fill(1)
            fill(7)

        @pl.when(block == 1)
        def _():
            send_plane(1)
            send_plane(7)
            forward(1, 0)

        @pl.when(block == 3)
        def _():
            forward(1, 1)

        @pl.when(block == 5)
        def _():
            forward(1, 2)

        return carry

    lax.fori_loop(0, QB, comp_loop, 0)

    forward(1, 3)
    fill(2)
    fill(6)
    forward(2, 0)
    send_plane(2)
    send_plane(6)
    forward(2, 1)
    forward(2, 2)
    forward(2, 3)
    fill(3)
    fill(5)
    forward(3, 0)
    send_plane(3)
    send_plane(5)
    forward(3, 1)
    forward(3, 2)
    forward(3, 3)
    fill(4)
    send_plane(4)
    for plane in (0, 1, 7, 2, 6, 3, 5, 4):
        for offset in range(1, NC):
            x_copy(plane, NC - offset).wait_recv()

    def selected_block(block, carry):
        for pair in range(TOPK // 2):
            first = incoming[pos_ref[block, 2 * pair]]
            second = incoming[pos_ref[block, 2 * pair + 1]]
            lanes = slice(pair * LANES, (pair + 1) * LANES)
            sel_kv[: KV // 2, lanes] = jnp.where(left_half, first, swap_halves(second))
            sel_kv[KV // 2 :, lanes] = jnp.where(left_half, swap_halves(first), second)
        scores = jnp.dot(queries_of(block), sel_kv[:DK, :], preferred_element_type=F32)
        _, weights, total = softmax(scores)
        result = lax.dot_general(
            weights.astype(BF16), sel_kv[DK:, :], nt, preferred_element_type=F32
        )
        result = result / total
        gates = gate_columns(block)
        first_row = pl.multiple_of(block * BLK, BLK)
        inside = (
            lax.broadcasted_iota(jnp.int32, (BLK, DV), 0) + c * ROWS + block * BLK < len_ref[0]
        )
        for head in range(HQ):
            rows = slice(head * BLK, (head + 1) * BLK)
            value = (
                mixed[block, rows, :] + result[rows] * gates[:, HQ + head : HQ + head + 1]
            )
            out_ref[pl.ds(first_row, BLK), head * DV : (head + 1) * DV] = jnp.where(
                inside, value, 0.0
            ).astype(BF16)
        return carry

    lax.fori_loop(0, QB, selected_block, 0)

    for offset in range(1, NZ):
        comp_over_z(offset).wait_send()
    for offset in range(1, NC):
        comp_over_c(offset).wait_send()
        ask(offset).wait_send()
        for plane in range(NZ):
            x_copy(plane, offset).wait_send()
    halo().wait_send()
    for step in range(4):
        for way in (1, -1):
            for chunk in z_chunks(way, step):
                z_copy(way, step, chunk).wait_send()


def attend(pos, length, q_rows, suffix_t, prefix_t, comp, requests, gates):
    anywhere = pl.BlockSpec(memory_space=pl.ANY)
    vmem = pl.BlockSpec(memory_space=pltpu.VMEM)
    smem = pl.BlockSpec(memory_space=pltpu.SMEM)
    plane = pltpu.VMEM((PAIRS, KV, LANES), BF16)
    slots = pltpu.VMEM((NZ * NC * CAP, KV // 2, LANES), BF16)
    dma = pltpu.SemaphoreType.DMA
    return pl.pallas_call(
        layer_kernel,
        name="layer",
        out_shape=jax.ShapeDtypeStruct((ROWS, HQ * DV), BF16),
        in_specs=[smem, smem, anywhere, anywhere, anywhere, anywhere, anywhere, vmem],
        out_specs=vmem,
        scratch_shapes=[plane] * 8
        + [
            slots,
            slots,
            pltpu.VMEM((NC, NZ, NB, 3 * LANES), BF16),
            pltpu.VMEM((KV, 2 * ROWS), BF16),
            pltpu.VMEM((NC, NZ, LANES), jnp.int32),
            pltpu.SMEM((NC, NZ, LANES), jnp.int32),
            pltpu.VMEM((ROWS, HQ * DK), BF16),
            pltpu.VMEM((HQ, ROWS, DK), BF16),
            pltpu.VMEM((QB, TILE, DV), F32),
            pltpu.VMEM((KV, TOPK * BLK), BF16),
            dma((PAIRS,)),
            dma((4,)),
            dma((2, 4, 4)),
            dma((2, 4, 4)),
            dma((NZ, NC)),
            dma((NZ, NC)),
            dma((2, NC)),
            dma((2, NC)),
            dma((NC,)),
            dma((NC,)),
            dma((NC,)),
            dma((1,)),
            dma((1,)),
        ],
        compiler_params=pltpu.CompilerParams(
            collective_id=0, has_side_effects=True, vmem_limit_bytes=60 * 1024 * 1024
        ),
    )(pos, length, q_rows, suffix_t, prefix_t, comp, requests, gates)


def shards(queries, suffix_kv, prefix_kv, pooling, gate_logits, selected, lengths, w_out):
    prefix_rows = prefix_kv.reshape(NB * BLK, KV)
    blocks = prefix_rows.reshape(NB, BLK, KV).astype(F32)
    comp_keys = jnp.einsum(
        "bjd,j->bd", blocks[:, :, :DK], pooling[0], precision=lax.Precision.HIGHEST
    )
    comp_values = jnp.einsum(
        "bjd,j->bd", blocks[:, :, DK:], pooling[1], precision=lax.Precision.HIGHEST
    )
    comp = jnp.concatenate(
        [comp_keys, jnp.zeros((NB, 2 * LANES - DK), F32), comp_values], axis=-1
    ).astype(BF16)

    z = lax.axis_index("sib")
    c = lax.axis_index("ctx")
    ids = selected.reshape(-1)
    owner = ids // NB
    local = ids % NB
    plane = (owner // NC - z + NZ) % NZ
    offset = (owner % NC - c + NC) % NC
    place = offset * NZ + plane
    order = jnp.arange(ids.shape[0], dtype=jnp.int32)
    rank = jnp.sum(
        ((place[:, None] == place[None, :]) & (order[None, :] < order[:, None])).astype(jnp.int32),
        axis=1,
    )
    pos = ((plane * NC + offset) * CAP + rank).reshape(QB, TOPK)
    lanes = jnp.arange(LANES, dtype=jnp.int32)
    entry = jnp.where(lanes[None, :] < CAP, local[:, None] // 2, local[:, None] % 2)
    hit = (place[:, None, None] == jnp.arange(NC * NZ, dtype=jnp.int32)[None, :, None]) & (
        (rank[:, None] == lanes[None, :]) | (rank[:, None] + CAP == lanes[None, :])
    )[:, None, :]
    requests = jnp.sum(jnp.where(hit, entry[:, None, :], 0), axis=0).reshape(NC, NZ, LANES)

    gates = jax.nn.sigmoid(gate_logits.reshape(ROWS, 3 * HQ))
    head_flat = attend(
        pos,
        lengths,
        queries.reshape(ROWS, HQ * DK),
        suffix_kv.reshape(ROWS, KV).T,
        prefix_rows.T,
        comp,
        requests,
        gates,
    )
    summed = lax.psum_scatter(
        jnp.dot(head_flat, w_out, preferred_element_type=F32),
        "head",
        scatter_dimension=0,
        tiled=True,
    )
    return summed.astype(BF16).reshape(1, -1, DM)


def solution(mesh):
    return jax.shard_map(
        shards,
        mesh=mesh,
        in_specs=(
            P("sib", "ctx", "head", None),
            P("sib", "ctx", "head", None),
            P(("sib", "ctx"), "head", None),
            P(),
            P("sib", "ctx", "head", None),
            P("sib", "ctx", "head", None),
            P("sib"),
            P("head", None),
        ),
        out_specs=P("sib", ("ctx", "head"), None),
        check_vma=False,
    )
```

time: 389 us -> 246 us (0.63)
  Pallas kernels: 0 us -> 155 us
  waiting for transfers between devices: 198 us -> 55.7 us
  matrix products: 66.2 us -> 10.4 us
  other arithmetic: 46.9 us -> 8.13 us
  local copies, waits for them, and re-layouts: 40.4 us -> 2.74 us
  starting transfers between devices: 22.7 us -> 0.01 us
    pallas_call x0 -> x1, Pallas kernels: none -> 155 us  [attend(): pl.pallas_call(layer_kernel, name='layer', out_shape=jax.ShapeDtypeStruct...]
    all_to_all x2 -> x0, waiting for transfers between devices: 67.8 us -> none  [the longest x1 60.3 us: shards(): lax.all_to_all(served, ('sib', 'ctx'), split_axis=0, concat_axis=0, tiled...]
    all_gather x1 -> x0, waiting for transfers between devices: 55.9 us -> none  [shards(): segment = lax.all_gather(compressed, ('sib', 'ctx'), axis=0, tiled=True)]
    dot_general x9 -> x3, matrix products: 66.2 us -> 10.4 us  [the longest x1 8.01 us: shards(): jnp.dot(head_flat, w_out, preferred_element_type=F32)]
    gather x3 -> x0, local copies, waits for them, and re-layouts: 26 us -> none  [the longest x2 16 us: shards(): jnp.take(received.reshape(owner_count * capacity, BLK, DK + DV), slot_pla...]
    reduce_sum x5 -> x2, other arithmetic: 26.9 us -> 2.21 us  [the longest x1 2.04 us: shards(): jnp.sum(jnp.where(hit, entry[:, None, :], 0), axis=0).reshape(NC, NZ, LANES)]
    all_to_all x2 -> x0, starting transfers between devices: 18.9 us -> none  [the longest x1 13 us: shards(): lax.all_to_all(requests, ('sib', 'ctx'), split_axis=0, concat_axis=0, til...]
    ppermute x1 -> x0, waiting for transfers between devices: 14.4 us -> none  [passed_along(): lax.ppermute(value, axis, [(source, source + steps) for source in range(f...]
  transfers between devices with their start and end apart: 5 -> 1, of which waited for: 5 -> 1; matrix products, arithmetic and copies ran while one was open for 20% -> 0% of each run, Pallas kernels for 0% -> 0%
where the time goes in v1:
time: 246 us
  Pallas kernels  155 us (63%)
  waiting for transfers between devices  55.7 us (23%)
  between operations  14.1 us (6%)
  matrix products  10.4 us (4%)
  other arithmetic  8.13 us (3%)
  local copies, waits for them, and re-layouts  2.74 us (1%)
    pallas_call x1, Pallas kernels, attend(): pl.pallas_call(layer_kernel, name='layer', out_shape=jax.ShapeDtypeStruct...  155 us
    reduce_scatter x1, waiting for transfers between devices, shards(): lax.psum_scatter(jnp.dot(head_flat, w_out, preferred_element_type=F32), '...  55.6 us
    dot_general x1, matrix products, shards(): jnp.dot(head_flat, w_out, preferred_element_type=F32)  8.01 us
  transfers between devices with their start and end apart: 1, of which 1 were waited for; matrix products, arithmetic and copies ran while one was open for 0% of the time, Pallas kernels for 0%

profile of v1, /device:TPU:1, one launch (start us, length us, event | category | flops | bytes accessed | tf_op | source)
XLA Modules:
  0.0 246.1 jit_solution(8678010875475118165)
XLA Ops:
  6.5 0.0 copy-start.1
  6.5 0.0 copy-start
  6.5 0.0 reduce-scatter.2.cloned.1.call-start
  6.6 0.5 broadcast.664
  7.1 1.3 reduce.3
  8.4 0.1 reshape.457
  8.6 0.2 convert_reduce_fusion
  8.7 0.1 reduce_sum.21
  8.8 0.1 iota_compare_fusion.2
  8.9 1.9 copy.14
  10.8 1.1 fusion.2
  11.9 1.2 fusion
  13.8 0.1 fusion.5
  13.9 0.0 copy-done
  13.9 0.1 copy.15
  14.0 0.8 divide_bitcast_fusion.gate_ref
  14.8 0.1 pad.1.clone
  14.9 0.0 copy-done.1
  14.9 0.6 fusion.13.pos_ref
  15.5 0.1 broadcast_select_fusion
  15.6 2.0 select_reduce_fusion
  17.7 0.6 pad_maximum_fusion.comp_ref
  18.3 155.1 %layer.1 = bf16[512,1024]{1,0:T(8,128)(2,1)} custom-call(s32[8,16]{1,0:T(8,128)} %fusion.13.pos_ref, s32[1]{0:T(128)S(6)} %copy.22.len_ref, bf16[512,1536]{1,0:T(8,128)(2,1)} %bitcast.34, bf16[320,512]{1,0:T(8,128)(2,1)} %bitcast.35, bf16[320,2048]{1,0:T(8,128)(2,1)} %bitcast.33, bf16[32,384]{1,0:T(8,128)(2,1)} %pad_maximum_fusion.comp_ref, ...), custom_call_target="tpu_custom_call" | custom-call | tf_op jit(solution)/shard_map/layer/pallas_call | solution.py:445
  173.4 8.0 %fusion.29 = f32[512,2560]{1,0:T(8,128)} fusion(bf16[512,1024]{1,0:T(8,128)(2,1)} %layer.1, bf16[1024,2560]{1,0:T(8,128)(2,1)} %param.15), kind=kOutput, calls=%fused_computation.80 | convolution fusion | flops 2684354560 | bytes 11534336 | tf_op jit(solution)/shard_map/dot_general | solution.py:529
  181.4 0.0 reduce-scatter.2.cloned.1.call-update
  181.4 55.6 %reduce-scatter.2.cloned.1.call-done = f32[128,2560]{1,0:T(8,128)} async-done(((f32[512,2560]{1,0:T(8,128)}), f32[128,2560]{1,0:T(8,128)}) %reduce-scatter.2.cloned.1.call-update) | async-done | bytes 1310736 | tf_op jit(solution)/shard_map/reduce_scatter | solution.py:528
  237.0 2.2 convert_bitcast_fusion
  (7 shorter events, 0.1 us)
Async XLA Ops:
  6.5 8.4 %copy-start.1 = (s32[1,8,1,16]{3,2,1,0:T(1,128)S(1)}, s32[1,8,1,16]{3,2,1,0:T(1,128)}, u32[]{:S(2)}) copy-start(s32[1,8,1,16]{3,2,1,0:T(1,128)} %param.13) | copy-start | bytes 1540
  6.5 7.4 %copy-start = (f32[1,512,1,24]{1,3,2,0:T(8,128)S(1)}, f32[1,512,1,24]{1,3,2,0:T(8,128)}, u32[]{:S(2)}) copy-start(f32[1,512,1,24]{1,3,2,0:T(8,128)} %param.12) | copy-start | bytes 147460
  6.5 230.5 %reduce-scatter.2.cloned.1.call-start = ((), (), s32[]{:S(2)}) async-start(), calls=%async_computation.1 | async-start | bytes 6553600 | tf_op jit(solution)/shard_map/reduce_scatter | solution.py:528
Sparse Core Ops, SparseCore 0:
  181.5 55.4 reduce-scatter.1

commit v2 on v1

--- a/solution.py
+++ b/solution.py
@@ -25,6 +25,12 @@
 CHUNK = 4
 LANES = 128
 TILE = HQ * BLK
+NY = 4
+OUT_ROWS = ROWS // NY
+GROUP_ROWS = HQ * DV
+HALF = GROUP_ROWS // 2
+PIECE = HALF // 4
+NTILE = 256
 SCALE2 = DK ** (-0.5) * 1.4426950408889634
 MESH = pl.DeviceIdType.MESH
 BF16 = jnp.bfloat16
@@ -47,14 +53,14 @@
 
 
 def layer_kernel(
-    pos_ref,
     len_ref,
+    id_ref,
+    pool_ref,
+    gate_ref,
     q_ref,
     suffix_ref,
     prefix_ref,
-    comp_ref,
-    request_ref,
-    gate_ref,
+    w_ref,
     out_ref,
     own,
     plus1,
@@ -68,12 +74,20 @@
     incoming,
     comp_all,
     near,
+    ask_table,
     asked,
     asked_smem,
+    place_table,
+    place_smem,
     q_raw,
     q_heads,
+    gates_all,
     mixed,
     sel_kv,
+    w_all,
+    heads_out,
+    heads_in,
+    partial,
     load_sem,
     misc_sem,
     z_send,
@@ -87,6 +101,12 @@
     ask_load,
     halo_send,
     halo_recv,
+    w_send,
+    w_recv,
+    twin_send,
+    twin_recv,
+    head_send,
+    head_recv,
 ):
     z = lax.axis_index("sib")
     c = lax.axis_index("ctx")
@@ -97,12 +117,20 @@
 
     def c_peer(offset):
         return (z, (c + offset) % NC, y)
+
+    def y_peer(offset):
+        return (z, c, (y + offset) % NY)
+
+    core = c % 2
+    twin_device = (z, c + 1 - 2 * core, y)
 
     barrier = pltpu.get_barrier_semaphore()
     for offset in range(1, NZ):
         pl.semaphore_signal(barrier, inc=1, device_id=z_peer(offset), device_id_type=MESH)
     for offset in range(1, NC):
         pl.semaphore_signal(barrier, inc=1, device_id=c_peer(offset), device_id_type=MESH)
+    for offset in range(1, NY):
+        pl.semaphore_signal(barrier, inc=1, device_id=y_peer(offset), device_id_type=MESH)
 
     loads = [
         pltpu.make_async_copy(
@@ -116,15 +144,13 @@
     q_load.start()
     near_load = pltpu.make_async_copy(suffix_ref, near.at[:, pl.ds(ROWS, ROWS)], misc_sem.at[1])
     near_load.start()
-    comp_load = pltpu.make_async_copy(comp_ref, comp_all.at[0, 0], misc_sem.at[2])
-    comp_load.start()
-    ask_self = pltpu.make_async_copy(request_ref.at[0], asked_smem.at[0], ask_load.at[0])
-    ask_self.start()
-    pl.semaphore_wait(barrier, NZ - 1 + NC - 1)
+    w_load = pltpu.make_async_copy(w_ref, w_all.at[0], misc_sem.at[2])
+    w_load.start()
+    pl.semaphore_wait(barrier, NZ - 1 + NC - 1 + NY - 1)
 
     def comp_over_z(offset):
         return remote(
-            comp_ref,
+            comp_all.at[0, 0],
             comp_all.at[0, NZ - offset],
             comp_send.at[0, offset],
             comp_recv.at[0, NZ - offset],
@@ -142,7 +168,7 @@
 
     def ask(offset):
         return remote(
-            request_ref.at[offset],
+            ask_table.at[offset],
             asked.at[NC - offset],
             ask_send.at[offset],
             ask_recv.at[NC - offset],
@@ -172,9 +198,71 @@
             z_peer(way),
         )
 
+    room = {0: 0, 1: 1, 7: 2, 2: 3, 6: 0, 3: 1, 5: 2, 4: 3}
+    room_before = {6: 0, 3: 1, 5: 7, 4: 2}
+
+    def w_copy(way, step, piece):
+        row = 0 if way == 1 else 1
+        rows = pl.ds(pl.multiple_of(core * HALF + piece * PIECE, PIECE), PIECE)
+        near_slot = 3 if way == 1 else 1
+        return remote(
+            w_ref.at[rows] if step == 0 else w_all.at[near_slot, rows],
+            w_all.at[near_slot if step == 0 else 2, rows],
+            w_send.at[row, step, piece],
+            w_recv.at[row, step, piece],
+            y_peer(way),
+        )
+
+    def w_pieces(way, step):
+        if step == 0:
+            return (0, 1, 2, 3) if way == 1 else (2, 3, 0, 1)
+        return (0, 1) if way == 1 else (2, 3)
+
+    def twin_copy(slot, piece):
+        rows = pl.ds(pl.multiple_of(core * HALF + piece * PIECE, PIECE), PIECE)
+        return remote(
+            w_all.at[slot, rows],
+            w_all.at[slot, rows],
+            twin_send.at[slot, piece],
+            twin_recv.at[slot, piece],
+            twin_device,
+        )
+
+    def twin_arrival(slot, piece):
+        rows = pl.ds(pl.multiple_of((1 - core) * HALF + piece * PIECE, PIECE), PIECE)
+        return remote(
+            w_all.at[slot, rows],
+            w_all.at[slot, rows],
+            twin_send.at[slot, piece],
+            twin_recv.at[slot, piece],
+            twin_device,
+        )
+
+    def w_service(step, turn):
+        for way in (1, -1):
+            piece = w_pieces(way, step)[turn]
+            w_copy(way, step, piece).wait_recv()
+            if step == 0 and piece in w_pieces(way, 1):
+                w_copy(way, 1, piece).start()
+            if step == 0:
+                twin_copy(3 if way == 1 else 1, piece).start()
+
+    def w_far_twins(turn):
+        for way in (1, -1):
+            twin_copy(2, w_pieces(way, 1)[turn]).start()
+
+    def head_copy(offset):
+        return remote(
+            heads_out.at[offset],
+            heads_in.at[NY - offset],
+            head_send.at[offset],
+            head_recv.at[NY - offset],
+            y_peer(offset),
+        )
+
     def x_copy(plane, offset):
         return remote(
-            outgoing.at[pl.ds((plane * NC + offset) * CAP, CAP)],
+            outgoing.at[pl.ds((room[plane] * NC + offset) * CAP, CAP)],
             incoming.at[pl.ds((plane * NC + NC - offset) * CAP, CAP)],
             x_send.at[plane, offset],
             x_recv.at[plane, NC - offset],
@@ -187,6 +275,9 @@
 
     def fill(plane):
         held = planes[plane]
+        if plane in room_before:
+            for offset in range(1, NC):
+                x_copy(room_before[plane], offset).wait_send()
 
         def one(index, carry):
             offset = index // CAP
@@ -199,12 +290,11 @@
             first = half == 0
             kept_upper = jnp.where(first, upper, swap_halves(upper))
             kept_lower = jnp.where(first, swap_halves(lower), lower)
-            outgoing[plane * NC * CAP + index] = jnp.where(left_half, kept_upper, kept_lower)
+            outgoing[room[plane] * NC * CAP + index] = jnp.where(left_half, kept_upper, kept_lower)
             return carry
 
         lax.fori_loop(0, NC * CAP, one, 0)
-        base = plane * NC * CAP
-        incoming[pl.ds(base, CAP)] = outgoing[pl.ds(base, CAP)]
+        incoming[pl.ds(plane * NC * CAP, CAP)] = outgoing[pl.ds(room[plane] * NC * CAP, CAP)]
 
     def send_plane(plane):
         for offset in (2, 6, 4, 3, 5, 1, 7):
@@ -217,33 +307,119 @@
                 if step < 3 and chunk in z_chunks(way, step + 1):
                     z_copy(way, step + 1, chunk).start()
 
-    for offset in (4, 3, 5, 2, 6, 1, 7):
-        comp_over_z(offset).start()
+    nt = (((1,), (1,)), ((), ()))
+
+    halo().start()
+    for way in (1, -1):
+        w_copy(way, 0, w_pieces(way, 0)[0]).start()
+    for load in loads:
+        load.wait()
+    for way in (1, -1):
+        z_copy(way, 0, 0).start()
+
+    ids = id_ref[...]
+    owner = ids // NB
+    local = ids % NB
+    plane_of = (owner // NC - z + NZ) % NZ
+    offset_of = (owner % NC - c + NC) % NC
+    place = offset_of * NZ + plane_of
+    square = (LANES, LANES)
+    down = lax.broadcasted_iota(jnp.int32, square, 0)
+    along = lax.broadcasted_iota(jnp.int32, square, 1)
+    place_along = jnp.broadcast_to(place, square)
+    place_down = jnp.sum(jnp.where(down == along, place_along, 0), axis=1, keepdims=True)
+    rank = jnp.sum(
+        jnp.where((place_down == place_along) & (down < along), 1, 0), axis=0, keepdims=True
+    )
+    landing = (plane_of * NC + offset_of) * CAP + jnp.minimum(rank, CAP - 1)
+    place_table[...] = jnp.broadcast_to(landing, (8, LANES))
+    wide = (NC * NZ, LANES)
+    matches = lax.broadcasted_iota(jnp.int32, wide, 0) == place
+    lane = lax.broadcasted_iota(jnp.int32, wide, 1)
+    table = jnp.zeros(wide, jnp.int32)
+    for slot in range(CAP):
+        hit = matches & (rank == slot)
+        pair_value = jnp.sum(jnp.where(hit, local // 2, 0), axis=1, keepdims=True)
+        half_value = jnp.sum(jnp.where(hit, local % 2, 0), axis=1, keepdims=True)
+        table = jnp.where(lane == slot, pair_value, table)
+        table = jnp.where(lane == CAP + slot, half_value, table)
+    ask_table[...] = table.reshape(NC, NZ, LANES)
+
+    rows3 = 3 * NB
+    down3 = lax.broadcasted_iota(jnp.int32, (rows3, LANES), 0)
+    along3 = lax.broadcasted_iota(jnp.int32, (rows3, LANES), 1)
+
+    def parts_of(row):
+        weights = jnp.concatenate([pool_ref[row : row + 1, :]] * 2, axis=1)
+        high = weights.astype(BF16).astype(F32)
+        middle = (weights - high).astype(BF16).astype(F32)
+        low = weights - high - middle
+        return jnp.where(down3 < NB, high, jnp.where(down3 < 2 * NB, middle, low))
+
+    key_parts = parts_of(0)
+    value_parts = parts_of(1)
+
+    def compress(pair, sums):
+        mine = down3 % NB == 2 * pair + along3 // BLK
+        tile = own[pair]
+        keys = lax.dot_general(
+            jnp.where(mine, key_parts, 0.0).astype(BF16),
+            tile[:DK],
+            nt,
+            preferred_element_type=F32,
+        )
+        values = lax.dot_general(
+            jnp.where(mine, value_parts, 0.0).astype(BF16),
+            tile[DK:],
+            nt,
+            preferred_element_type=F32,
+        )
+        return sums[0] + keys, sums[1] + values
+
+    key_sums, value_sums = lax.fori_loop(
+        0, PAIRS, compress, (jnp.zeros((rows3, DK), F32), jnp.zeros((rows3, DV), F32))
+    )
+    comp_all[0, 0, :, :DK] = (
+        key_sums[:NB] + key_sums[NB : 2 * NB] + key_sums[2 * NB :]
+    ).astype(BF16)
+    comp_all[0, 0, :, DK : 2 * LANES] = jnp.zeros((NB, 2 * LANES - DK), BF16)
+    comp_all[0, 0, :, 2 * LANES :] = (
+        value_sums[:NB] + value_sums[NB : 2 * NB] + value_sums[2 * NB :]
+    ).astype(BF16)
+
     for offset in range(1, NC):
         ask(offset).start()
-    halo().start()
-    for load in loads:
-        load.wait()
-    for chunk in range(4):
-        for way in (1, -1):
-            z_copy(way, 0, chunk).start()
-
+    ask_self = pltpu.make_async_copy(ask_table.at[0], asked_smem.at[0], ask_load.at[0])
+    ask_self.start()
+    place_copy = pltpu.make_async_copy(place_table, place_smem, misc_sem.at[3])
+    place_copy.start()
+
+    gates_all[...] = jax.nn.sigmoid(gate_ref[...]).T
     q_load.wait()
     for head in range(HQ):
         q_heads[head] = q_raw[:, head * DK : (head + 1) * DK]
 
+    for offset in (4, 3, 5, 2, 6, 1, 7):
+        comp_over_z(offset).start()
+    for chunk in range(1, 4):
+        for way in (1, -1):
+            z_copy(way, 0, chunk).start()
+    for turn in range(1, 4):
+        for way in (1, -1):
+            w_copy(way, 0, w_pieces(way, 0)[turn]).start()
+
     for offset in range(1, NC):
         ask(NC - offset).wait_recv()
         pltpu.make_async_copy(asked.at[offset], asked_smem.at[offset], ask_load.at[offset]).start()
-    comp_load.wait()
+    for offset in range(1, NC):
+        pltpu.make_async_copy(asked.at[offset], asked_smem.at[offset], ask_load.at[offset]).wait()
+    ask_self.wait()
+    place_copy.wait()
+    fill(0)
     for offset in range(1, NZ):
         comp_over_z(NZ - offset).wait_recv()
     for offset in (4, 2, 6, 3, 5, 1, 7):
         comp_over_c(offset).start()
-    for offset in range(1, NC):
-        pltpu.make_async_copy(asked.at[offset], asked_smem.at[offset], ask_load.at[offset]).wait()
-    ask_self.wait()
-    fill(0)
 
     def queries_of(block):
         rows = pl.ds(pl.multiple_of(block * BLK, BLK), BLK)
@@ -251,7 +427,7 @@
 
     def gate_columns(block):
         rows = pl.ds(pl.multiple_of(block * BLK, BLK), BLK)
-        return gate_ref[rows, :]
+        return gates_all[rows, :]
 
     def softmax(scores, previous_max=None):
         top = jnp.max(scores, axis=-1, keepdims=True)
@@ -259,8 +435,6 @@
             top = jnp.maximum(previous_max, top)
         weights = jnp.exp2(scores * SCALE2 - top * SCALE2)
         return top, weights, jnp.sum(weights, axis=-1, keepdims=True)
-
-    nt = (((1,), (1,)), ((), ()))
 
     near_load.wait()
     halo().wait_recv()
@@ -297,6 +471,8 @@
         @pl.when(block == 2)
         def _():
             forward(0, 0)
+
+            w_service(0, 0)
 
         @pl.when(block == 4)
         def _():
@@ -349,6 +525,7 @@
             forward(0, 3)
             fill(1)
             fill(7)
+            w_service(0, 1)
 
         @pl.when(block == 1)
         def _():
@@ -359,6 +536,7 @@
         @pl.when(block == 3)
         def _():
             forward(1, 1)
+            w_service(0, 2)
 
         @pl.when(block == 5)
         def _():
@@ -371,10 +549,13 @@
     forward(1, 3)
     fill(2)
     fill(6)
+    w_service(0, 3)
     forward(2, 0)
     send_plane(2)
     send_plane(6)
     forward(2, 1)
+    w_service(1, 0)
+    w_far_twins(0)
     forward(2, 2)
     forward(2, 3)
     fill(3)
@@ -382,22 +563,33 @@
     forward(3, 0)
     send_plane(3)
     send_plane(5)
+    forward(3, 2)
+    w_service(1, 1)
     forward(3, 1)
-    forward(3, 2)
     forward(3, 3)
     fill(4)
+    w_load.wait()
     send_plane(4)
+    w_far_twins(1)
     for plane in (0, 1, 7, 2, 6, 3, 5, 4):
         for offset in range(1, NC):
             x_copy(plane, NC - offset).wait_recv()
 
-    def selected_block(block, carry):
+    def selected_block(turn, carry):
+        target = NY - 1 - turn // 2
+        block = 2 * ((y + target) % NY) + turn % 2
         for pair in range(TOPK // 2):
-            first = incoming[pos_ref[block, 2 * pair]]
-            second = incoming[pos_ref[block, 2 * pair + 1]]
+            first = incoming[place_smem[0, block * TOPK + 2 * pair]]
+            second = incoming[place_smem[0, block * TOPK + 2 * pair + 1]]
             lanes = slice(pair * LANES, (pair + 1) * LANES)
             sel_kv[: KV // 2, lanes] = jnp.where(left_half, first, swap_halves(second))
             sel_kv[KV // 2 :, lanes] = jnp.where(left_half, swap_halves(first), second)
+        for peer in range(1, NY):
+
+            @pl.when(turn == 2 * (NY - peer))
+            def _():
+                head_copy(peer).start()
+
         scores = jnp.dot(queries_of(block), sel_kv[:DK, :], preferred_element_type=F32)
         _, weights, total = softmax(scores)
         result = lax.dot_general(
@@ -405,7 +597,7 @@
         )
         result = result / total
         gates = gate_columns(block)
-        first_row = pl.multiple_of(block * BLK, BLK)
+        first_row = pl.multiple_of((turn % 2) * BLK, BLK)
         inside = (
             lax.broadcasted_iota(jnp.int32, (BLK, DV), 0) + c * ROWS + block * BLK < len_ref[0]
         )
@@ -414,52 +606,92 @@
             value = (
                 mixed[block, rows, :] + result[rows] * gates[:, HQ + head : HQ + head + 1]
             )
-            out_ref[pl.ds(first_row, BLK), head * DV : (head + 1) * DV] = jnp.where(
+            heads_out[target, pl.ds(first_row, BLK), head * DV : (head + 1) * DV] = jnp.where(
                 inside, value, 0.0
             ).astype(BF16)
         return carry
 
     lax.fori_loop(0, QB, selected_block, 0)
+
+    for slot in range(1, NY):
+        for piece in range(4):
+            twin_arrival(slot, piece).wait_recv()
+    for peer in (3, 2):
+        head_copy(peer).wait_recv()
+
+    def project_near(index, carry):
+        columns = pl.ds(pl.multiple_of(index * NTILE, NTILE), NTILE)
+        total = jnp.dot(heads_out[0], w_all[0, :, columns], preferred_element_type=F32)
+        total += jnp.dot(heads_in[1], w_all[1, :, columns], preferred_element_type=F32)
+        total += jnp.dot(heads_in[2], w_all[2, :, columns], preferred_element_type=F32)
+        partial[:, columns] = total
+        return carry
+
+    lax.fori_loop(0, DM // NTILE, project_near, 0)
+    head_copy(1).wait_recv()
+
+    def project_last(index, carry):
+        columns = pl.ds(pl.multiple_of(index * NTILE, NTILE), NTILE)
+        total = jnp.dot(heads_in[3], w_all[3, :, columns], preferred_element_type=F32)
+        out_ref[:, columns] = (partial[:, columns] + total).astype(BF16)
+        return carry
+
+    lax.fori_loop(0, DM // NTILE, project_last, 0)
 
     for offset in range(1, NZ):
         comp_over_z(offset).wait_send()
     for offset in range(1, NC):
         comp_over_c(offset).wait_send()
         ask(offset).wait_send()
-        for plane in range(NZ):
+        for plane in (6, 3, 5, 4):
             x_copy(plane, offset).wait_send()
     halo().wait_send()
+    for way in (1, -1):
+        for step in range(2):
+            for piece in w_pieces(way, step):
+                w_copy(way, step, piece).wait_send()
+    for slot in range(1, NY):
+        head_copy(slot).wait_send()
+        for piece in range(4):
+            twin_copy(slot, piece).wait_send()
     for step in range(4):
         for way in (1, -1):
             for chunk in z_chunks(way, step):
                 z_copy(way, step, chunk).wait_send()
 
 
-def attend(pos, length, q_rows, suffix_t, prefix_t, comp, requests, gates):
+def shards(queries, suffix_kv, prefix_kv, pooling, gate_logits, selected, lengths, w_out):
     anywhere = pl.BlockSpec(memory_space=pl.ANY)
     vmem = pl.BlockSpec(memory_space=pltpu.VMEM)
     smem = pl.BlockSpec(memory_space=pltpu.SMEM)
     plane = pltpu.VMEM((PAIRS, KV, LANES), BF16)
-    slots = pltpu.VMEM((NZ * NC * CAP, KV // 2, LANES), BF16)
     dma = pltpu.SemaphoreType.DMA
-    return pl.pallas_call(
+    out = pl.pallas_call(
         layer_kernel,
         name="layer",
-        out_shape=jax.ShapeDtypeStruct((ROWS, HQ * DV), BF16),
-        in_specs=[smem, smem, anywhere, anywhere, anywhere, anywhere, anywhere, vmem],
+        out_shape=jax.ShapeDtypeStruct((OUT_ROWS, DM), BF16),
+        in_specs=[smem, vmem, vmem, vmem, anywhere, anywhere, anywhere, anywhere],
         out_specs=vmem,
         scratch_shapes=[plane] * 8
         + [
-            slots,
-            slots,
+            pltpu.VMEM((4 * NC * CAP, KV // 2, LANES), BF16),
+            pltpu.VMEM((NZ * NC * CAP, KV // 2, LANES), BF16),
             pltpu.VMEM((NC, NZ, NB, 3 * LANES), BF16),
             pltpu.VMEM((KV, 2 * ROWS), BF16),
             pltpu.VMEM((NC, NZ, LANES), jnp.int32),
+            pltpu.VMEM((NC, NZ, LANES), jnp.int32),
             pltpu.SMEM((NC, NZ, LANES), jnp.int32),
+            pltpu.VMEM((8, LANES), jnp.int32),
+            pltpu.SMEM((8, LANES), jnp.int32),
             pltpu.VMEM((ROWS, HQ * DK), BF16),
             pltpu.VMEM((HQ, ROWS, DK), BF16),
+            pltpu.VMEM((ROWS, 3 * HQ), F32),
             pltpu.VMEM((QB, TILE, DV), F32),
             pltpu.VMEM((KV, TOPK * BLK), BF16),
+            pltpu.VMEM((NY, GROUP_ROWS, DM), BF16),
+            pltpu.VMEM((NY, OUT_ROWS, GROUP_ROWS), BF16),
+            pltpu.VMEM((NY, OUT_ROWS, GROUP_ROWS), BF16),
+            pltpu.VMEM((OUT_ROWS, DM), F32),
             dma((PAIRS,)),
             dma((4,)),
             dma((2, 4, 4)),
@@ -473,65 +705,27 @@
             dma((NC,)),
             dma((1,)),
             dma((1,)),
+            dma((2, 2, 4)),
+            dma((2, 2, 4)),
+            dma((NY, 4)),
+            dma((NY, 4)),
+            dma((NY,)),
+            dma((NY,)),
         ],
         compiler_params=pltpu.CompilerParams(
-            collective_id=0, has_side_effects=True, vmem_limit_bytes=60 * 1024 * 1024
+            collective_id=0, has_side_effects=True, vmem_limit_bytes=67_043_328
         ),
-    )(pos, length, q_rows, suffix_t, prefix_t, comp, requests, gates)
-
-
-def shards(queries, suffix_kv, prefix_kv, pooling, gate_logits, selected, lengths, w_out):
-    prefix_rows = prefix_kv.reshape(NB * BLK, KV)
-    blocks = prefix_rows.reshape(NB, BLK, KV).astype(F32)
-    comp_keys = jnp.einsum(
-        "bjd,j->bd", blocks[:, :, :DK], pooling[0], precision=lax.Precision.HIGHEST
-    )
-    comp_values = jnp.einsum(
-        "bjd,j->bd", blocks[:, :, DK:], pooling[1], precision=lax.Precision.HIGHEST
-    )
-    comp = jnp.concatenate(
-        [comp_keys, jnp.zeros((NB, 2 * LANES - DK), F32), comp_values], axis=-1
-    ).astype(BF16)
-
-    z = lax.axis_index("sib")
-    c = lax.axis_index("ctx")
-    ids = selected.reshape(-1)
-    owner = ids // NB
-    local = ids % NB
-    plane = (owner // NC - z + NZ) % NZ
-    offset = (owner % NC - c + NC) % NC
-    place = offset * NZ + plane
-    order = jnp.arange(ids.shape[0], dtype=jnp.int32)
-    rank = jnp.sum(
-        ((place[:, None] == place[None, :]) & (order[None, :] < order[:, None])).astype(jnp.int32),
-        axis=1,
-    )
-    pos = ((plane * NC + offset) * CAP + rank).reshape(QB, TOPK)
-    lanes = jnp.arange(LANES, dtype=jnp.int32)
-    entry = jnp.where(lanes[None, :] < CAP, local[:, None] // 2, local[:, None] % 2)
-    hit = (place[:, None, None] == jnp.arange(NC * NZ, dtype=jnp.int32)[None, :, None]) & (
-        (rank[:, None] == lanes[None, :]) | (rank[:, None] + CAP == lanes[None, :])
-    )[:, None, :]
-    requests = jnp.sum(jnp.where(hit, entry[:, None, :], 0), axis=0).reshape(NC, NZ, LANES)
-
-    gates = jax.nn.sigmoid(gate_logits.reshape(ROWS, 3 * HQ))
-    head_flat = attend(
-        pos,
+    )(
         lengths,
+        selected.reshape(1, QB * TOPK),
+        pooling,
+        gate_logits.reshape(ROWS, 3 * HQ).T,
         queries.reshape(ROWS, HQ * DK),
         suffix_kv.reshape(ROWS, KV).T,
-        prefix_rows.T,
-        comp,
-        requests,
-        gates,
+        prefix_kv.reshape(NB * BLK, KV).T,
+        w_out,
     )
-    summed = lax.psum_scatter(
-        jnp.dot(head_flat, w_out, preferred_element_type=F32),
-        "head",
-        scatter_dimension=0,
-        tiled=True,
-    )
-    return summed.astype(BF16).reshape(1, -1, DM)
+    return out.reshape(1, OUT_ROWS, DM)
 
 
 def solution(mesh):

time: 246 us -> 172 us (0.70)
  waiting for transfers between devices: 55.7 us -> 0 us
  between operations: 14.1 us -> 0.66 us
  Pallas kernels: 155 us -> 167 us
  matrix products: 10.4 us -> 0 us
  other arithmetic: 8.13 us -> 1.35 us
    reduce_scatter x1 -> x0, waiting for transfers between devices: 55.6 us -> none  [shards(): lax.psum_scatter(jnp.dot(head_flat, w_out, preferred_element_type=F32), '...]
    pallas_call x1, Pallas kernels: 155 us -> 167 us  [shards(): pl.pallas_call(layer_kernel, name='layer', out_shape=jax.ShapeDtypeStruct...]
    dot_general x3 -> x0, matrix products: 10.4 us -> none  [the longest x1 8.01 us: shards(): jnp.dot(head_flat, w_out, preferred_element_type=F32)]
  transfers between devices with their start and end apart: 1 -> 0, of which waited for: 1 -> 0; matrix products, arithmetic and copies ran while one was open for 0% -> 0% of each run, Pallas kernels for 0% -> 0%
where the time goes in v2:
time: 172 us
  Pallas kernels  167 us (97%)
  local copies, waits for them, and re-layouts  3.07 us (2%)
    pallas_call x1, Pallas kernels, shards(): pl.pallas_call(layer_kernel, name='layer', out_shape=jax.ShapeDtypeStruct...  167 us

profile of v2, /device:TPU:1, one launch (start us, length us, event | category | flops | bytes accessed | tf_op | source)
XLA Modules:
  0.0 171.9 jit_solution(2900151488893197334)
XLA Ops:
  0.7 0.5 broadcast.3
  1.2 1.3 reduce.3
  2.5 0.6 reshape.18.id_ref
  3.1 166.8 %layer.1 = bf16[128,2560]{1,0:T(8,128)(2,1)} custom-call(s32[1]{0:T(128)S(6)} %copy.10.len_ref, s32[1,128]{1,0:T(1,128)} %reshape.18.id_ref, f32[2,64]{1,0:T(2,128)} %pool_ref.1, f32[24,512]{1,0:T(8,128)} %bitcast.15, bf16[512,1536]{1,0:T(8,128)(2,1)} %bitcast.12, bf16[320,512]{1,0:T(8,128)(2,1)} %bitcast.14, bf16[320,2048]{1,0:T(8,128)(2,1)} %bitcast.13, ...), custom_call_target="tpu_custom_call" | custom-call | tf_op jit(solution)/shard_map/layer/pallas_call | solution.py:669
  169.9 2.0 %copy.11 = bf16[1,128,2560]{2,1,0:T(8,128)(2,1)} copy(bf16[1,128,2560]{2,1,0:T(8,128)(2,1)} %bitcast.11) | data formatting | bytes 1310720

commit v3 on v2

--- a/solution.py
+++ b/solution.py
@@ -26,6 +26,7 @@
 LANES = 128
 TILE = HQ * BLK
 NY = 4
+NX = 4
 OUT_ROWS = ROWS // NY
 GROUP_ROWS = HQ * DV
 HALF = GROUP_ROWS // 2
@@ -157,19 +158,28 @@
             z_peer(offset),
         )
 
-    def comp_over_c(offset):
+    def comp_over_c(chips):
         return remote(
             comp_all.at[0],
-            comp_all.at[NC - offset],
-            comp_send.at[1, offset],
-            comp_recv.at[1, NC - offset],
-            c_peer(offset),
+            comp_all.at[NX - chips],
+            comp_send.at[1, chips],
+            comp_recv.at[1, NX - chips],
+            c_peer(2 * chips),
+        )
+
+    def comp_to_twin(slot):
+        return remote(
+            comp_all.at[slot],
+            comp_all.at[NX + slot],
+            comp_send.at[1, NX + slot],
+            comp_recv.at[1, NX + slot],
+            twin_device,
         )
 
     def ask(offset):
         return remote(
-            ask_table.at[offset],
-            asked.at[NC - offset],
+            ask_table.at[pl.ds(offset, 1)],
+            asked.at[pl.ds(NC - offset, 1)],
             ask_send.at[offset],
             ask_recv.at[NC - offset],
             c_peer(offset),
@@ -251,12 +261,13 @@
         for way in (1, -1):
             twin_copy(2, w_pieces(way, 1)[turn]).start()
 
-    def head_copy(offset):
-        return remote(
-            heads_out.at[offset],
-            heads_in.at[NY - offset],
-            head_send.at[offset],
-            head_recv.at[NY - offset],
+    def head_copy(offset, part):
+        rows = pl.ds(part * BLK, BLK)
+        return remote(
+            heads_out.at[offset, rows],
+            heads_in.at[NY - offset, rows],
+            head_send.at[offset, part],
+            head_recv.at[NY - offset, part],
             y_peer(offset),
         )
 
@@ -273,32 +284,41 @@
 
     planes = {0: own, 7: plus1, 6: plus2, 5: plus3, 1: minus1, 2: minus2, 3: minus3, 4: far}
 
-    def fill(plane):
+    def exchange(plane):
         held = planes[plane]
         if plane in room_before:
             for offset in range(1, NC):
                 x_copy(room_before[plane], offset).wait_send()
 
-        def one(index, carry):
-            offset = index // CAP
-            slot = index % CAP
-            pair = asked_smem[offset, plane, slot]
-            half = asked_smem[offset, plane, CAP + slot]
-            tile = held[pair]
-            upper = tile[: KV // 2]
-            lower = tile[KV // 2 :]
-            first = half == 0
-            kept_upper = jnp.where(first, upper, swap_halves(upper))
-            kept_lower = jnp.where(first, swap_halves(lower), lower)
-            outgoing[room[plane] * NC * CAP + index] = jnp.where(left_half, kept_upper, kept_lower)
+        def peer_at(turn):
+            offset = turn * 0
+            for index, value in enumerate((4, 5, 3, 2, 6, 7, 1)):
+                offset = jnp.where(turn == index, value, offset)
+            return offset
+
+        def serve(turn, carry):
+            offset = peer_at(turn)
+            for slot in range(CAP):
+                pair = asked_smem[offset, plane * 8 + slot]
+                half = asked_smem[offset, plane * 8 + CAP + slot]
+                tile = held[pair]
+                upper = tile[: KV // 2]
+                lower = tile[KV // 2 :]
+                first = half == 0
+                kept_upper = jnp.where(first, upper, swap_halves(upper))
+                kept_lower = jnp.where(first, swap_halves(lower), lower)
+                outgoing[(room[plane] * NC + offset) * CAP + slot] = jnp.where(
+                    left_half, kept_upper, kept_lower
+                )
+
+            @pl.when(turn >= 1)
+            def _():
+                x_copy(plane, peer_at(turn - 1)).start()
+
             return carry
 
-        lax.fori_loop(0, NC * CAP, one, 0)
+        lax.fori_loop(0, NC, serve, 0)
         incoming[pl.ds(plane * NC * CAP, CAP)] = outgoing[pl.ds(room[plane] * NC * CAP, CAP)]
-
-    def send_plane(plane):
-        for offset in (2, 6, 4, 3, 5, 1, 7):
-            x_copy(plane, offset).start()
 
     def forward(step, chunk):
         for way in (1, -1):
@@ -314,10 +334,11 @@
         w_copy(way, 0, w_pieces(way, 0)[0]).start()
     for load in loads:
         load.wait()
-    for way in (1, -1):
-        z_copy(way, 0, 0).start()
-
-    ids = id_ref[...]
+    for chunk in range(3):
+        for way in (1, -1):
+            z_copy(way, 0, chunk).start()
+
+    ids = jnp.concatenate([id_ref[0, block] for block in range(QB)], axis=1)
     owner = ids // NB
     local = ids % NB
     plane_of = (owner // NC - z + NZ) % NZ
@@ -337,13 +358,14 @@
     matches = lax.broadcasted_iota(jnp.int32, wide, 0) == place
     lane = lax.broadcasted_iota(jnp.int32, wide, 1)
     table = jnp.zeros(wide, jnp.int32)
+    own_lanes = lane // 8 == lax.broadcasted_iota(jnp.int32, wide, 0) % NZ
     for slot in range(CAP):
         hit = matches & (rank == slot)
         pair_value = jnp.sum(jnp.where(hit, local // 2, 0), axis=1, keepdims=True)
         half_value = jnp.sum(jnp.where(hit, local % 2, 0), axis=1, keepdims=True)
-        table = jnp.where(lane == slot, pair_value, table)
-        table = jnp.where(lane == CAP + slot, half_value, table)
-    ask_table[...] = table.reshape(NC, NZ, LANES)
+        table = jnp.where(own_lanes & (lane % 8 == slot), pair_value, table)
+        table = jnp.where(own_lanes & (lane % 8 == CAP + slot), half_value, table)
+    ask_table[...] = jnp.sum(table.reshape(NC, NZ, LANES), axis=1)
 
     rows3 = 3 * NB
     down3 = lax.broadcasted_iota(jnp.int32, (rows3, LANES), 0)
@@ -389,37 +411,33 @@
 
     for offset in range(1, NC):
         ask(offset).start()
-    ask_self = pltpu.make_async_copy(ask_table.at[0], asked_smem.at[0], ask_load.at[0])
+    ask_self = pltpu.make_async_copy(
+        ask_table.at[pl.ds(0, 1)], asked.at[pl.ds(0, 1)], ask_load.at[0]
+    )
     ask_self.start()
     place_copy = pltpu.make_async_copy(place_table, place_smem, misc_sem.at[3])
     place_copy.start()
-
     gates_all[...] = jax.nn.sigmoid(gate_ref[...]).T
+    for offset in (4, 3, 5, 2, 6, 1, 7):
+        comp_over_z(offset).start()
+    for way in (1, -1):
+        z_copy(way, 0, 3).start()
+    for turn in range(1, 4):
+        for way in (1, -1):
+            w_copy(way, 0, w_pieces(way, 0)[turn]).start()
+
     q_load.wait()
     for head in range(HQ):
         q_heads[head] = q_raw[:, head * DK : (head + 1) * DK]
 
-    for offset in (4, 3, 5, 2, 6, 1, 7):
-        comp_over_z(offset).start()
-    for chunk in range(1, 4):
-        for way in (1, -1):
-            z_copy(way, 0, chunk).start()
-    for turn in range(1, 4):
-        for way in (1, -1):
-            w_copy(way, 0, w_pieces(way, 0)[turn]).start()
-
     for offset in range(1, NC):
         ask(NC - offset).wait_recv()
-        pltpu.make_async_copy(asked.at[offset], asked_smem.at[offset], ask_load.at[offset]).start()
-    for offset in range(1, NC):
-        pltpu.make_async_copy(asked.at[offset], asked_smem.at[offset], ask_load.at[offset]).wait()
     ask_self.wait()
+    ask_all = pltpu.make_async_copy(asked, asked_smem, ask_load.at[1])
+    ask_all.start()
+    ask_all.wait()
     place_copy.wait()
-    fill(0)
-    for offset in range(1, NZ):
-        comp_over_z(NZ - offset).wait_recv()
-    for offset in (4, 2, 6, 3, 5, 1, 7):
-        comp_over_c(offset).start()
+    exchange(0)
 
     def queries_of(block):
         rows = pl.ds(pl.multiple_of(block * BLK, BLK), BLK)
@@ -462,9 +480,6 @@
             )
         return carry
 
-    window_block(0, 0)
-    send_plane(0)
-
     def window_loop(block, carry):
         window_block(block, carry)
 
@@ -472,22 +487,30 @@
         def _():
             forward(0, 0)
 
-            w_service(0, 0)
-
-        @pl.when(block == 4)
+        @pl.when(block == 5)
         def _():
             forward(0, 1)
 
-        @pl.when(block == 6)
-        def _():
-            forward(0, 2)
-
         return carry
 
-    lax.fori_loop(1, QB, window_loop, 0)
-
-    for offset in range(1, NC):
-        comp_over_c(NC - offset).wait_recv()
+    lax.fori_loop(0, QB, window_loop, 0)
+
+    for offset in range(1, NZ):
+        comp_over_z(NZ - offset).wait_recv()
+    for chips in (2, 1, 3):
+        comp_over_c(chips).start()
+    comp_to_twin(0).start()
+    forward(0, 2)
+    w_service(0, 0)
+    forward(0, 3)
+    exchange(1)
+    exchange(7)
+    for chips in (1, 3, 2):
+        comp_over_c(NX - chips).wait_recv()
+        comp_to_twin(chips).start()
+    w_service(0, 1)
+    for slot in range(NX):
+        comp_to_twin(slot).wait_recv()
 
     half_keys = NZ * NC * NB // 2
 
@@ -522,61 +545,51 @@
 
         @pl.when(block == 0)
         def _():
-            forward(0, 3)
-            fill(1)
-            fill(7)
-            w_service(0, 1)
-
-        @pl.when(block == 1)
-        def _():
-            send_plane(1)
-            send_plane(7)
             forward(1, 0)
 
-        @pl.when(block == 3)
+        @pl.when(block == 2)
         def _():
             forward(1, 1)
-            w_service(0, 2)
-
-        @pl.when(block == 5)
+
+        @pl.when(block == 4)
         def _():
             forward(1, 2)
+            w_service(0, 2)
+
+        @pl.when(block == 6)
+        def _():
+            forward(1, 3)
+            exchange(2)
+            exchange(6)
 
         return carry
 
     lax.fori_loop(0, QB, comp_loop, 0)
 
-    forward(1, 3)
-    fill(2)
-    fill(6)
     w_service(0, 3)
     forward(2, 0)
-    send_plane(2)
-    send_plane(6)
     forward(2, 1)
     w_service(1, 0)
     w_far_twins(0)
     forward(2, 2)
     forward(2, 3)
-    fill(3)
-    fill(5)
+    exchange(3)
+    exchange(5)
     forward(3, 0)
-    send_plane(3)
-    send_plane(5)
     forward(3, 2)
     w_service(1, 1)
     forward(3, 1)
     forward(3, 3)
-    fill(4)
+    exchange(4)
     w_load.wait()
-    send_plane(4)
     w_far_twins(1)
     for plane in (0, 1, 7, 2, 6, 3, 5, 4):
         for offset in range(1, NC):
             x_copy(plane, NC - offset).wait_recv()
 
     def selected_block(turn, carry):
-        target = NY - 1 - turn // 2
+        group = turn // 2
+        target = jnp.where(group == 0, 2, jnp.where(group == 1, 3, jnp.where(group == 2, 1, 0)))
         block = 2 * ((y + target) % NY) + turn % 2
         for pair in range(TOPK // 2):
             first = incoming[place_smem[0, block * TOPK + 2 * pair]]
@@ -584,11 +597,11 @@
             lanes = slice(pair * LANES, (pair + 1) * LANES)
             sel_kv[: KV // 2, lanes] = jnp.where(left_half, first, swap_halves(second))
             sel_kv[KV // 2 :, lanes] = jnp.where(left_half, swap_halves(first), second)
-        for peer in range(1, NY):
-
-            @pl.when(turn == 2 * (NY - peer))
+        for done in range(QB - 2):
+
+            @pl.when(turn == done + 1)
             def _():
-                head_copy(peer).start()
+                head_copy((2, 3, 1)[done // 2], done % 2).start()
 
         scores = jnp.dot(queries_of(block), sel_kv[:DK, :], preferred_element_type=F32)
         _, weights, total = softmax(scores)
@@ -616,23 +629,25 @@
     for slot in range(1, NY):
         for piece in range(4):
             twin_arrival(slot, piece).wait_recv()
-    for peer in (3, 2):
-        head_copy(peer).wait_recv()
+    for part in range(2):
+        head_copy(2, part).wait_recv()
 
     def project_near(index, carry):
         columns = pl.ds(pl.multiple_of(index * NTILE, NTILE), NTILE)
         total = jnp.dot(heads_out[0], w_all[0, :, columns], preferred_element_type=F32)
-        total += jnp.dot(heads_in[1], w_all[1, :, columns], preferred_element_type=F32)
         total += jnp.dot(heads_in[2], w_all[2, :, columns], preferred_element_type=F32)
         partial[:, columns] = total
         return carry
 
     lax.fori_loop(0, DM // NTILE, project_near, 0)
-    head_copy(1).wait_recv()
+    for peer in (3, 1):
+        for part in range(2):
+            head_copy(peer, part).wait_recv()
 
     def project_last(index, carry):
         columns = pl.ds(pl.multiple_of(index * NTILE, NTILE), NTILE)
-        total = jnp.dot(heads_in[3], w_all[3, :, columns], preferred_element_type=F32)
+        total = jnp.dot(heads_in[1], w_all[1, :, columns], preferred_element_type=F32)
+        total += jnp.dot(heads_in[3], w_all[3, :, columns], preferred_element_type=F32)
         out_ref[:, columns] = (partial[:, columns] + total).astype(BF16)
         return carry
 
@@ -641,17 +656,21 @@
     for offset in range(1, NZ):
         comp_over_z(offset).wait_send()
     for offset in range(1, NC):
-        comp_over_c(offset).wait_send()
         ask(offset).wait_send()
         for plane in (6, 3, 5, 4):
             x_copy(plane, offset).wait_send()
     halo().wait_send()
+    for chips in range(1, NX):
+        comp_over_c(chips).wait_send()
+    for slot in range(NX):
+        comp_to_twin(slot).wait_send()
     for way in (1, -1):
         for step in range(2):
             for piece in w_pieces(way, step):
                 w_copy(way, step, piece).wait_send()
     for slot in range(1, NY):
-        head_copy(slot).wait_send()
+        for part in range(2):
+            head_copy(slot, part).wait_send()
         for piece in range(4):
             twin_copy(slot, piece).wait_send()
     for step in range(4):
@@ -678,9 +697,9 @@
             pltpu.VMEM((NZ * NC * CAP, KV // 2, LANES), BF16),
             pltpu.VMEM((NC, NZ, NB, 3 * LANES), BF16),
             pltpu.VMEM((KV, 2 * ROWS), BF16),
-            pltpu.VMEM((NC, NZ, LANES), jnp.int32),
-            pltpu.VMEM((NC, NZ, LANES), jnp.int32),
-            pltpu.SMEM((NC, NZ, LANES), jnp.int32),
+            pltpu.VMEM((NC, LANES), jnp.int32),
+            pltpu.VMEM((NC, LANES), jnp.int32),
+            pltpu.SMEM((NC, LANES), jnp.int32),
             pltpu.VMEM((8, LANES), jnp.int32),
             pltpu.SMEM((8, LANES), jnp.int32),
             pltpu.VMEM((ROWS, HQ * DK), BF16),
@@ -702,22 +721,22 @@
             dma((2, NC)),
             dma((NC,)),
             dma((NC,)),
-            dma((NC,)),
+            dma((2,)),
             dma((1,)),
             dma((1,)),
             dma((2, 2, 4)),
             dma((2, 2, 4)),
             dma((NY, 4)),
             dma((NY, 4)),
-            dma((NY,)),
-            dma((NY,)),
+            dma((NY, 2)),
+            dma((NY, 2)),
         ],
         compiler_params=pltpu.CompilerParams(
             collective_id=0, has_side_effects=True, vmem_limit_bytes=67_043_328
         ),
     )(
         lengths,
-        selected.reshape(1, QB * TOPK),
+        selected,
         pooling,
         gate_logits.reshape(ROWS, 3 * HQ).T,
         queries.reshape(ROWS, HQ * DK),

time: 172 us -> 160 us (0.930)
  Pallas kernels: 167 us -> 157 us
    pallas_call x1, Pallas kernels: 167 us -> 157 us  [shards(): pl.pallas_call(layer_kernel, name='layer', out_shape=jax.ShapeDtypeStruct...]
where the time goes in v3:
time: 160 us
  Pallas kernels  157 us (98%)
  local copies, waits for them, and re-layouts  1.97 us (1%)
    pallas_call x1, Pallas kernels, shards(): pl.pallas_call(layer_kernel, name='layer', out_shape=jax.ShapeDtypeStruct...  157 us

profile of v3, /device:TPU:1, one launch (start us, length us, event | category | flops | bytes accessed | tf_op | source)
XLA Modules:
  0.0 159.7 jit_solution(6645280842047931429)
XLA Ops:
  0.7 157.1 %layer.1 = bf16[128,2560]{1,0:T(8,128)(2,1)} custom-call(s32[1]{0:T(128)S(6)} %copy.10.len_ref, s32[1,8,1,16]{3,2,1,0:T(1,128)} %id_ref.1, f32[2,64]{1,0:T(2,128)} %pool_ref.1, f32[24,512]{1,0:T(8,128)} %bitcast.15, bf16[512,1536]{1,0:T(8,128)(2,1)} %bitcast.12, bf16[320,512]{1,0:T(8,128)(2,1)} %bitcast.14, bf16[320,2048]{1,0:T(8,128)(2,1)} %bitcast.13, ...), custom_call_target="tpu_custom_call" | custom-call | tf_op jit(solution)/shard_map/layer/pallas_call | solution.py:688
  157.8 2.0 %copy.11 = bf16[1,128,2560]{2,1,0:T(8,128)(2,1)} copy(bf16[1,128,2560]{2,1,0:T(8,128)(2,1)} %bitcast.11) | data formatting | bytes 1310720

commit v4 on v3

--- a/solution.py
+++ b/solution.py
@@ -27,6 +27,7 @@
 TILE = HQ * BLK
 NY = 4
 NX = 4
+NEAR_Z = (2, 6, 1, 7)
 OUT_ROWS = ROWS // NY
 GROUP_ROWS = HQ * DV
 HALF = GROUP_ROWS // 2
@@ -126,7 +127,7 @@
     twin_device = (z, c + 1 - 2 * core, y)
 
     barrier = pltpu.get_barrier_semaphore()
-    for offset in range(1, NZ):
+    for offset in NEAR_Z:
         pl.semaphore_signal(barrier, inc=1, device_id=z_peer(offset), device_id_type=MESH)
     for offset in range(1, NC):
         pl.semaphore_signal(barrier, inc=1, device_id=c_peer(offset), device_id_type=MESH)
@@ -147,7 +148,7 @@
     near_load.start()
     w_load = pltpu.make_async_copy(w_ref, w_all.at[0], misc_sem.at[2])
     w_load.start()
-    pl.semaphore_wait(barrier, NZ - 1 + NC - 1 + NY - 1)
+    pl.semaphore_wait(barrier, len(NEAR_Z) + NC - 1 + NY - 1)
 
     def comp_over_z(offset):
         return remote(
@@ -156,6 +157,25 @@
             comp_send.at[0, offset],
             comp_recv.at[0, NZ - offset],
             z_peer(offset),
+        )
+
+    def comp_relay(way):
+        return remote(
+            comp_all.at[0, (NZ - 2 * way) % NZ],
+            comp_all.at[0, (NZ - 3 * way) % NZ],
+            comp_send.at[0, 3 if way == 1 else 5],
+            comp_recv.at[0, 3 if way == 1 else 5],
+            z_peer(way),
+        )
+
+    def comp_far(way):
+        rows = pl.ds(0 if way == 1 else NB // 2, NB // 2)
+        return remote(
+            comp_all.at[0, (NZ - 2 * way) % NZ, rows],
+            comp_all.at[0, NZ // 2, rows],
+            comp_send.at[0, 4 if way == 1 else 0],
+            comp_recv.at[0, 4 if way == 1 else 0],
+            z_peer(2 * way),
         )
 
     def comp_over_c(chips):
@@ -418,7 +438,7 @@
     place_copy = pltpu.make_async_copy(place_table, place_smem, misc_sem.at[3])
     place_copy.start()
     gates_all[...] = jax.nn.sigmoid(gate_ref[...]).T
-    for offset in (4, 3, 5, 2, 6, 1, 7):
+    for offset in NEAR_Z:
         comp_over_z(offset).start()
     for way in (1, -1):
         z_copy(way, 0, 3).start()
@@ -495,20 +515,35 @@
 
     lax.fori_loop(0, QB, window_loop, 0)
 
-    for offset in range(1, NZ):
+    for offset in NEAR_Z:
         comp_over_z(NZ - offset).wait_recv()
-    for chips in (2, 1, 3):
-        comp_over_c(chips).start()
-    comp_to_twin(0).start()
+    for way in (1, -1):
+        comp_far(way).start()
+        comp_relay(way).start()
     forward(0, 2)
     w_service(0, 0)
     forward(0, 3)
     exchange(1)
     exchange(7)
+    w_service(0, 1)
+    forward(1, 0)
+    for way in (1, -1):
+        comp_far(way).wait_recv()
+        comp_relay(way).wait_recv()
+    for chips in (2, 1, 3):
+        comp_over_c(chips).start()
+    comp_to_twin(0).start()
+    forward(1, 1)
+    w_service(0, 2)
+    forward(1, 2)
+    forward(1, 3)
+    exchange(2)
+    exchange(6)
     for chips in (1, 3, 2):
         comp_over_c(NX - chips).wait_recv()
         comp_to_twin(chips).start()
-    w_service(0, 1)
+    w_service(0, 3)
+    forward(2, 0)
     for slot in range(NX):
         comp_to_twin(slot).wait_recv()
 
@@ -545,33 +580,18 @@
 
         @pl.when(block == 0)
         def _():
-            forward(1, 0)
-
-        @pl.when(block == 2)
-        def _():
-            forward(1, 1)
+            forward(2, 1)
+            w_service(1, 0)
+            w_far_twins(0)
 
         @pl.when(block == 4)
         def _():
-            forward(1, 2)
-            w_service(0, 2)
-
-        @pl.when(block == 6)
-        def _():
-            forward(1, 3)
-            exchange(2)
-            exchange(6)
+            forward(2, 2)
 
         return carry
 
     lax.fori_loop(0, QB, comp_loop, 0)
 
-    w_service(0, 3)
-    forward(2, 0)
-    forward(2, 1)
-    w_service(1, 0)
-    w_far_twins(0)
-    forward(2, 2)
     forward(2, 3)
     exchange(3)
     exchange(5)
@@ -640,21 +660,33 @@
         return carry
 
     lax.fori_loop(0, DM // NTILE, project_near, 0)
-    for peer in (3, 1):
-        for part in range(2):
-            head_copy(peer, part).wait_recv()
+    for part in range(2):
+        head_copy(3, part).wait_recv()
+
+    def project_next(index, carry):
+        columns = pl.ds(pl.multiple_of(index * NTILE, NTILE), NTILE)
+        partial[:, columns] += jnp.dot(
+            heads_in[1], w_all[1, :, columns], preferred_element_type=F32
+        )
+        return carry
+
+    lax.fori_loop(0, DM // NTILE, project_next, 0)
+    for part in range(2):
+        head_copy(1, part).wait_recv()
 
     def project_last(index, carry):
         columns = pl.ds(pl.multiple_of(index * NTILE, NTILE), NTILE)
-        total = jnp.dot(heads_in[1], w_all[1, :, columns], preferred_element_type=F32)
-        total += jnp.dot(heads_in[3], w_all[3, :, columns], preferred_element_type=F32)
+        total = jnp.dot(heads_in[3], w_all[3, :, columns], preferred_element_type=F32)
         out_ref[:, columns] = (partial[:, columns] + total).astype(BF16)
         return carry
 
     lax.fori_loop(0, DM // NTILE, project_last, 0)
 
-    for offset in range(1, NZ):
+    for offset in NEAR_Z:
         comp_over_z(offset).wait_send()
+    for way in (1, -1):
+        comp_far(way).wait_send()
+        comp_relay(way).wait_send()
     for offset in range(1, NC):
         ask(offset).wait_send()
         for plane in (6, 3, 5, 4):

time: 160 us -> 159 us (level)
  no operation moved by 1% of the time
where the time goes in v4:
time: 159 us
  Pallas kernels  156 us (98%)
  local copies, waits for them, and re-layouts  1.97 us (1%)
    pallas_call x1, Pallas kernels, shards(): pl.pallas_call(layer_kernel, name='layer', out_shape=jax.ShapeDtypeStruct...  156 us

profile of v4, /device:TPU:1, one launch (start us, length us, event | category | flops | bytes accessed | tf_op | source)
XLA Modules:
  0.0 159.0 jit_solution(18042853599197122646)
XLA Ops:
  0.7 156.4 %layer.1 = bf16[128,2560]{1,0:T(8,128)(2,1)} custom-call(s32[1]{0:T(128)S(6)} %copy.10.len_ref, s32[1,8,1,16]{3,2,1,0:T(1,128)} %id_ref.1, f32[2,64]{1,0:T(2,128)} %pool_ref.1, f32[24,512]{1,0:T(8,128)} %bitcast.15, bf16[512,1536]{1,0:T(8,128)(2,1)} %bitcast.12, bf16[320,512]{1,0:T(8,128)(2,1)} %bitcast.14, bf16[320,2048]{1,0:T(8,128)(2,1)} %bitcast.13, ...), custom_call_target="tpu_custom_call" | custom-call | tf_op jit(solution)/shard_map/layer/pallas_call | solution.py:720
  157.0 2.0 %copy.11 = bf16[1,128,2560]{2,1,0:T(8,128)(2,1)} copy(bf16[1,128,2560]{2,1,0:T(8,128)(2,1)} %bitcast.11) | data formatting | bytes 1310720
